TPU v7x, 128 devices: a whole 4x4x4 slice. The times are simulated.
128 devices in a mesh: aa: 16 (over x, z), ba: 8 (over y, core).
Axes of the slice: x: 4, y: 4, z: 4, core: 2. Of those that a mesh axis runs over, the one named last changes fastest.
Arguments:
- tokens: bfloat16 [16384, 1024], P(('aa', 'ba')), may hold values from -24 to 24, as said below
- attn_gain: float32 [1024], replicated, may hold values from 0.25 to 1.75
- w_query: bfloat16 [1024, 1024], replicated, may hold values from -0.1875 to 0.1875
- w_key: bfloat16 [1024, 1024], replicated, may hold values from -0.1875 to 0.1875
- w_value: bfloat16 [1024, 1024], replicated, may hold values from -0.1875 to 0.1875
- head_gain: float32 [1024], P('ba'), may hold values from 0.25 to 1.75
- w_output: bfloat16 [1024, 1024], replicated, may hold values from -0.1875 to 0.1875
- mlp_gain: float32 [1024], replicated, may hold values from 0.25 to 1.75
- w_in: bfloat16 [1024, 4096], replicated, may hold values from -0.1875 to 0.1875
- w_out: bfloat16 [4096, 1024], replicated, may hold values from -0.09375 to 0.09375
Outputs:
- attended: bfloat16 [16384, 1024], P(('aa', 'ba'))
- result: bfloat16 [16384, 1024], P(('aa', 'ba'))
Inputs may be any that keep to these rules, and one draw needn't show every extreme that they name: `tokens`: entries have magnitude at most 24.
All inputs are finite; a program needn't handle non-finite values.
Results may differ from a plain program's by a relative error of at most 0.013.
Values may be sent and summed in bfloat16 or wider, within the bound.
No kernel may reach another device: no remote copies, remote signals or barrier semaphores. Data moves between devices by JAX's collectives and lax.ppermute only.
A program may use at most 128 MiB of HBM per device.

v0:
```python
import jax
import jax.numpy as jnp
from jax import lax
from jax.experimental import pallas as pl
from jax.experimental.pallas import tpu as pltpu
from jax.sharding import Mesh
from jax.sharding import PartitionSpec as P

D = 1024
FF = 4096
HS = 64
NF = HS * (HS + 1) // 2
PIECE = NF // 4
ROWS = 128
PAIR = 2 * ROWS
LEN = 1024
F32 = jnp.float32
BF = jnp.bfloat16
SPLIT = ("x", "z", "y", "c")
BA = ("y", "c")
MIB = 1 << 20


VM = pl.BlockSpec(memory_space=pltpu.VMEM)
HBM = pl.BlockSpec(memory_space=pltpu.HBM)
ANY = pl.BlockSpec(memory_space=pl.ANY)


def xor_pairs(n, k):
    return [(i, i ^ k) for i in range(n)]


def flip(index, k):
    return jnp.bitwise_xor(index, k) if k else index


def rms(matrix, gain):
    return matrix * lax.rsqrt(jnp.mean(matrix * matrix, axis=-1, keepdims=True) + 1e-05) * gain


def columns(k):
    return pl.multiple_of((2 * flip(lax.axis_index("y"), k) + lax.axis_index("c")) * 128, 128)


def load_kernel(tok, gain, wk, wv, normed, gout, wout, tbuf, sems, tsems):
    first = [
        pltpu.make_async_copy(gain, gout, tsems.at[0]),
        pltpu.make_async_copy(tok, tbuf, tsems.at[1]),
    ]
    for copy in first:
        copy.start()
    copies = []
    for k in range(1, 4):
        for j, w in enumerate((wk, wv)):
            copy = pltpu.make_async_copy(
                w.at[:, pl.ds(columns(k), 128)],
                wout.at[k - 1, :, j * 128 : (j + 1) * 128],
                sems.at[k - 1, j],
            )
            copy.start()
            copies.append(copy)
    for copy in first:
        copy.wait()
    normed[...] = rms(tbuf[...].astype(F32), gout[...]).astype(BF)
    for copy in copies:
        copy.wait()


def kv_kernel(own, other, gain, wkv, *rest):
    outs, normed = rest[:3], rest[3]
    c = lax.axis_index("c")
    normed[pl.ds(pl.multiple_of(c * ROWS, ROWS), ROWS), :] = own[...]
    at = pl.ds(pl.multiple_of((1 - c) * ROWS, ROWS), ROWS)
    normed[at, :] = rms(other[...].astype(F32), gain[...]).astype(BF)
    for k in range(3):
        outs[k][...] = jnp.dot(normed[...], wkv[k], preferred_element_type=F32).astype(BF)


def q_kernel(normed, wq, wk, wv, *rest):
    outs, own, wbuf, sems = rest[:4], rest[4], rest[5], rest[6]
    copies = []
    for j, w in enumerate((wk, wv)):
        copy = pltpu.make_async_copy(
            w.at[:, pl.ds(columns(0), 128)], wbuf.at[:, j * 128 : (j + 1) * 128], sems.at[j]
        )
        copy.start()
        copies.append(copy)
    for k in range(4):
        outs[k][...] = jnp.dot(
            normed[...], wq[:, pl.ds(columns(k), 128)], preferred_element_type=F32
        ).astype(BF)
    for copy in copies:
        copy.wait()
    own[...] = jnp.dot(normed[...], wbuf[...], preferred_element_type=F32).astype(BF)


MAIN = 8 * HS


def fill_queries(ext, h, phi, col):
    for d in range(32):
        row = MAIN * (d % 4) + HS * (d // 4)
        phi[row : row + HS, col : col + LEN] = (ext[h, 0:HS, :] * ext[h, d : d + HS, :]).astype(BF)
    phi[4 * MAIN : NF, col : col + LEN] = (ext[h, 0:32, :] * ext[h, 32:HS, :]).astype(BF)


def key_piece(ext, vz, phi, turned, k):
    c = flip(lax.axis_index("z"), k)
    for h in range(2):
        col = slice(h * LEN, (h + 1) * LEN)
        turned[...] = pltpu.roll(ext[h], lax.rem(2 * HS - c, 2 * HS), 0)
        for j in range(8):
            left = ext[h, 0:HS, :]
            twice = left + left
            if j == 0:
                twice = jnp.where(c == 0, left, twice)
            phi[j * HS : (j + 1) * HS, col] = (twice * turned[4 * j : 4 * j + HS, :]).astype(BF)
        low = ext[h, pl.ds(pl.multiple_of(8 * c, 8), 8), :]
        high = ext[h, pl.ds(pl.multiple_of(8 * c + 32, 8), 8), :]
        phi[MAIN:PIECE, col] = ((low + low) * high).astype(BF)
    return jnp.dot(phi[...], vz[...], preferred_element_type=F32).astype(BF)


def state_kernel(*refs):
    chunks, outs = refs[:4], refs[4:6]
    ext, vz, phi, turned = refs[6:]
    lane = lax.broadcasted_iota(jnp.int32, (PAIR, 128), 1)
    zero = jnp.zeros((PAIR, 128), BF)
    for k in range(4):
        at = slice(k * PAIR, (k + 1) * PAIR)
        keys = chunks[k][:, 0:128].astype(F32).T
        value = chunks[k][:, 128:256]
        for h in range(2):
            part = keys[h * HS : (h + 1) * HS]
            ext[h, 0:HS, at] = part
            ext[h, HS : 2 * HS, at] = part
            mine = (lane >= HS) if h else (lane < HS)
            vz[h * LEN + k * PAIR : h * LEN + (k + 1) * PAIR, :] = jnp.where(mine, value, zero)
    for out, k in zip(outs, (1, 2)):
        out[...] = key_piece(ext, vz, phi, turned, k)


def third_kernel(ext, vz, out, phi, turned):
    out[...] = key_piece(ext, vz, phi, turned, 3)


def rest_kernel(ext, vz, after, out, phi, turned):
    out[...] = key_piece(ext, vz, phi, turned, 0)


def pair_rows(k):
    return pl.ds(pl.multiple_of(flip(lax.axis_index("y"), k) * PAIR, PAIR), PAIR)


def inside_kernel(*refs):
    pairs, queries, out = refs[:4], refs[4:8], refs[8]
    q, kk, v = refs[9:]
    for k in range(4):
        at = pair_rows(k)
        q[at, :] = queries[k][...]
        kk[at, :] = pairs[k][:, 0:128]
        v[at, :] = pairs[k][:, 128:256]
    T = 256
    lane_q = lax.broadcasted_iota(jnp.int32, (T, 128), 1)
    lane_v = lax.broadcasted_iota(jnp.int32, (LEN, 128), 1)
    causal = lax.broadcasted_iota(jnp.int32, (T, T), 0) >= lax.broadcasted_iota(
        jnp.int32, (T, T), 1
    )
    nt = (((1,), (1,)), ((), ()))
    vh = [jnp.where((lane_v >= HS) if h else (lane_v < HS), v[...], jnp.zeros((), BF)) for h in range(2)]
    for i in range(LEN // T):
        rows = slice(i * T, (i + 1) * T)
        total = None
        for h in range(2):
            qh = jnp.where((lane_q >= HS) if h else (lane_q < HS), q[rows, :], jnp.zeros((), BF))
            last = lax.dot_general(qh, kk[rows, :], nt, preferred_element_type=F32)
            last = jnp.where(causal, last * last, 0.0).astype(BF)
            add = jnp.dot(last, vh[h][rows], preferred_element_type=F32)
            total = add if total is None else total + add
            if i:
                full = lax.dot_general(qh, kk[0 : i * T, :], nt, preferred_element_type=F32)
                full = (full * full).astype(BF)
                total = total + jnp.dot(full, vh[h][0 : i * T], preferred_element_type=F32)
        out[rows, :] = total


def total_kernel(*refs):
    pieces, out = refs[:4], refs[4]
    out[...] = sum(p[...].astype(F32) for p in pieces).astype(BF)


def combine_kernel(*refs):
    pieces, totals, outs = refs[:4], refs[4:8], refs[10:14]
    x, z = lax.axis_index("x"), lax.axis_index("z")
    base = jnp.zeros((PIECE, 128), F32)
    for k in range(1, 4):
        base = base + jnp.where(flip(x, k) < x, totals[k][...].astype(F32), 0.0)
    for k in range(4):
        acc = base
        for j in range(4):
            if j != k:
                acc = acc + jnp.where(flip(z, j) < flip(z, k), pieces[j][...].astype(F32), 0.0)
        outs[k][...] = acc.astype(BF)


def features_kernel(*refs):
    queries, phi, ext = refs[:4], refs[4], refs[5]
    for k in range(4):
        at = slice(k * PAIR, (k + 1) * PAIR)
        turned = queries[k][...].astype(F32).T
        for h in range(2):
            part = turned[h * HS : (h + 1) * HS]
            ext[h, 0:HS, at] = part
            ext[h, HS : 2 * HS, at] = part
    for h in range(2):
        fill_queries(ext, h, phi, h * LEN)


def attend(turned, phi, inside, gain, first, last):
    halves = [
        jnp.dot(
            turned[h * HS : (h + 1) * HS],
            phi[:, h * LEN + first * PAIR : h * LEN + last * PAIR],
            preferred_element_type=F32,
        )
        for h in range(2)
    ]
    numer = jnp.concatenate(halves, axis=0).T
    low = lax.broadcasted_iota(jnp.int32, (PAIR, 128), 1) < HS
    outs = []
    for k in range(first, last):
        at = slice((k - first) * PAIR, (k - first + 1) * PAIR)
        mine = numer[at] + inside[pair_rows(k), :]
        square = mine * mine
        one = jnp.sum(jnp.where(low, square, 0.0), axis=-1, keepdims=True)
        two = jnp.sum(jnp.where(low, 0.0, square), axis=-1, keepdims=True)
        mean = jnp.where(low, one, two) * (1.0 / HS)
        outs.append((mine * lax.rsqrt(mean + 1e-05) * gain[...]).astype(BF))
    return outs


def apply_kernel(*refs):
    phi, states, inside, gain, outs, turned = refs[0], refs[1:5], refs[5], refs[6], refs[7:10], refs[10]
    state = refs[11]
    z = lax.axis_index("z")
    for k in range(4):
        c = flip(z, k)
        piece = states[k][...].astype(F32)
        state[pl.ds(pl.multiple_of(c * MAIN, MAIN), MAIN), :] = piece[0:MAIN]
        state[pl.ds(pl.multiple_of(4 * MAIN + 8 * c, 8), 8), :] = piece[MAIN:PIECE]
    turned[...] = state[...].T.astype(BF)
    for out, value in zip(outs, attend(turned[...], phi, inside, gain, 1, 4)):
        out[...] = value


def own_kernel(phi, turned, inside, gain, out):
    out[...] = attend(turned[...], phi, inside, gain, 0, 1)[0]


def merge_kernel(*refs):
    parts, out = refs[:4], refs[4]
    row = pl.multiple_of((1 - lax.axis_index("c")) * ROWS, ROWS)
    for k in range(4):
        col = pl.multiple_of(flip(lax.axis_index("y"), k) * 128, 128)
        out[:, pl.ds(col, 128)] = parts[k][pl.ds(row, ROWS), :]


FB = 2048


def mlp_kernel(*refs):
    parts, other, tok, gain, wo, wi, wf = refs[:4], *refs[4:10]
    att, res = refs[10:12]
    y, c = lax.axis_index("y"), lax.axis_index("c")
    row = pl.multiple_of(c * ROWS, ROWS)
    for k in range(4):
        col = pl.multiple_of((2 * flip(y, k) + c) * 128, 128)
        att[:, pl.ds(col, 128)] = parts[k][pl.ds(row, ROWS), :]
        col = pl.multiple_of((2 * k + 1 - c) * 128, 128)
        att[:, pl.ds(col, 128)] = other[:, k * 128 : (k + 1) * 128]
    stream = tok[...].astype(F32) + jnp.dot(att[...], wo[...], preferred_element_type=F32)
    stream = stream.astype(BF).astype(F32)
    normed = rms(stream, gain[...]).astype(BF)
    acc = stream
    for j in range(FF // FB):
        at = slice(j * FB, (j + 1) * FB)
        u = jnp.dot(normed, wi[:, at], preferred_element_type=F32)
        hidden = 0.5 * u * (1.0 + jnp.tanh(0.7978845608028654 * (u + 0.044715 * u * u * u)))
        acc = acc + jnp.dot(hidden.astype(BF), wf[at, :], preferred_element_type=F32)
    res[...] = acc.astype(BF)


def call(kernel, outs, scratch, specs, limit, flops=0, moved=0):
    return pl.pallas_call(
        kernel,
        out_shape=outs,
        in_specs=specs,
        out_specs=jax.tree.map(lambda _: VM, outs),
        scratch_shapes=scratch,
        compiler_params=pltpu.CompilerParams(vmem_limit_bytes=limit * MIB),
        cost_estimate=pl.CostEstimate(flops=flops, bytes_accessed=moved, transcendentals=0),
    )


def arr(*shape, dtype=BF):
    return jax.ShapeDtypeStruct(shape, dtype)


def fixed(array):
    return pltpu.with_memory_space_constraint(array, pltpu.HBM)


ORDER = (2, 3, 1)


def exchange(parts, axis):
    moved = {k: lax.ppermute(parts[k], axis, xor_pairs(4, k)) for k in ORDER}
    return [parts[0]] + [moved[k] for k in range(1, 4)]


def body(tokens, attn_gain, w_query, w_key, w_value, head_gain, w_output, mlp_gain, w_in, w_out):
    swapped = lax.ppermute(tokens, "c", xor_pairs(2, 1))
    own, gain, wkv = call(
        load_kernel,
        [arr(ROWS, D), arr(1, D, dtype=F32), arr(3, D, 256)],
        [
            pltpu.VMEM((ROWS, D), BF),
            pltpu.SemaphoreType.DMA((3, 2)),
            pltpu.SemaphoreType.DMA((2,)),
        ],
        [HBM] * 4,
        4,
        flops=128 * 1024 * 1024,
        moved=4 * MIB,
    )(fixed(tokens), fixed(attn_gain.reshape(1, D)), fixed(w_key), fixed(w_value))
    *pairs, normed = call(
        kv_kernel,
        [arr(PAIR, 256)] * 3 + [arr(PAIR, D)],
        [],
        [VM] * 4,
        6,
        flops=2 * 256 * 1024 * 1024,
        moved=3 * MIB,
    )(own, swapped, gain, wkv)
    pairs = exchange([None, *pairs], "y")
    *queries, pairs[0] = call(
        q_kernel,
        [arr(PAIR, 128)] * 4 + [arr(PAIR, 256)],
        [pltpu.VMEM((D, 256), BF), pltpu.SemaphoreType.DMA((2,))],
        [VM] * 2 + [HBM] * 2,
        6,
        flops=2 * 256 * 1024 * 512,
        moved=4 * MIB,
    )(normed, w_query, fixed(w_key), fixed(w_value))
    spare = [pltpu.VMEM((PIECE, 2 * LEN), BF), pltpu.VMEM((2 * HS, LEN), F32)]
    cost = 2 * PIECE * 2 * LEN * 256
    first, second, ext, vz = call(
        state_kernel,
        [arr(PIECE, 128)] * 2 + [arr(2, 2 * HS, LEN, dtype=F32), arr(2 * LEN, 128)],
        spare,
        [VM] * 4,
        8,
        flops=2 * cost,
        moved=2 * MIB,
    )(*pairs)
    third = call(third_kernel, arr(PIECE, 128), spare, [VM] * 2, 8, flops=cost, moved=MIB)(ext, vz)
    own = call(
        rest_kernel, arr(PIECE, 128), spare, [VM] * 2 + [ANY], 8, flops=cost, moved=MIB
    )(ext, vz, third)
    pieces = [own]
    for k, piece in ((1, first), (2, second), (3, third)):
        pieces.append(lax.ppermute(piece, "z", xor_pairs(4, k)))
    queries = lax.optimization_barrier((queries, third))[0]
    queries = exchange(queries, "y")
    inside = call(
        inside_kernel,
        arr(LEN, 128, dtype=F32),
        [pltpu.VMEM((LEN, 128), BF)] * 3,
        [VM] * 8,
        16,
        flops=2 * 1024 * 1024 * 256 * 2,
        moved=2 * MIB,
    )(*pairs, *queries)

    total = call(total_kernel, arr(PIECE, 128), [], [VM] * 4, 4, moved=MIB)(*pieces)
    moved = {k: lax.ppermute(total, "x", xor_pairs(4, k)) for k in ORDER}
    totals = [total] + [moved[k] for k in range(1, 4)]
    phi = call(
        features_kernel,
        arr(NF, 2 * LEN),
        [pltpu.VMEM((2, 2 * HS, LEN), F32)],
        [VM] * 4,
        6,
        flops=NF * 2 * LEN * 128,
        moved=9 * MIB,
    )(*queries)
    states = call(
        combine_kernel, [arr(PIECE, 128)] * 4, [], [VM] * 8 + [ANY] * 2, 8, moved=MIB
    )(*pieces, *totals, phi, inside)
    states = exchange(states, "z")

    scale = head_gain.reshape(1, 128)
    *parts, turned = call(
        apply_kernel,
        [arr(PAIR, 128)] * 3 + [arr(128, NF)],
        [pltpu.VMEM((NF, 128), F32)],
        [VM] * 7,
        12,
        flops=2 * NF * 2 * LEN * 192,
        moved=2 * MIB,
    )(phi, *states, inside, scale)
    moved = {k: lax.ppermute(parts[k - 1], "y", xor_pairs(4, k)) for k in ORDER}
    mine = call(
        own_kernel, arr(PAIR, 128), [], [VM] * 4, 8, flops=2 * NF * 2 * LEN * 64, moved=2 * MIB
    )(phi, turned, inside, scale)
    parts = [mine] + [moved[k] for k in range(1, 4)]
    other = call(merge_kernel, arr(ROWS, 512), [], [VM] * 4, 4)(*parts)
    other = lax.ppermute(other, "c", xor_pairs(2, 1))

    return call(
        mlp_kernel,
        [arr(ROWS, D)] * 2,
        [],
        [VM] * 10,
        8,
        flops=2 * 128 * 1024 * 9216,
        moved=18 * MIB,
    )(*parts, other, tokens, mlp_gain.reshape(1, D), w_output, w_in, w_out)


def solution(mesh):
    finer = Mesh(mesh.devices.reshape(4, 4, 4, 2), SPLIT)
    placed = (P(SPLIT, None), P(), P(), P(), P(), P(BA), P(), P(), P(), P())
    return jax.shard_map(
        body,
        mesh=finer,
        in_specs=placed,
        out_specs=(P(SPLIT, None), P(SPLIT, None)),
        check_vma=False,
    )
```

profile of v0, /device:TPU:1, one launch (start us, length us, event | category | flops | bytes accessed | tf_op | source)
XLA Modules:
  0.0 67.9 jit_solution(14656120765347246097)
XLA Ops:
  0.6 1.5 %collective-permute-start = (bf16[128,1024]{1,0:T(8,128)(2,1)}, bf16[128,1024]{1,0:T(8,128)(2,1)S(1)}, u32[]{:S(2)}, u32[]{:S(2)}) collective-permute-start(bf16[128,1024]{1,0:T(8,128)(2,1)} %refs_5_.1), channel_id=1, source_target_pairs={{0,1},{1,0},{2,3},{3,2},{4,5},{5,4},{6,7},{7,6},{8,9},{9,8},{10,11... | collective-permute-start | bytes 786440 | tf_op jit(solution)/shard_map/ppermute | solution.py:322
  2.1 1.6 %shard_map.113 = (bf16[128,1024]{1,0:T(8,128)(2,1)S(1)}, f32[1,1024]{1,0:T(1,128)S(1)}, bf16[3,1024,256]{2,1,0:T(8,128)(2,1)S(1)}) custom-call(bf16[128,1024]{1,0:T(8,128)(2,1)} %refs_5_.1, f32[1,1024]{1,0:T(1,128)} %bitcast.10, bf16[1024,1024]{1,0:T(8,128)(2,1)} %wk.3, bf16[1024,1024]{1,0:T(8,128)(2,1)} %wv.3), custom_call_target="tpu_custom_call" | custom-call | flops 134217728 | bytes 4194304 | tf_op jit(solution)/shard_map/pallas_call | solution.py:323
  4.4 1.5 %collective-permute-start.1 = (bf16[256,256]{1,0:T(8,128)(2,1)S(1)}, bf16[256,256]{1,0:T(8,128)(2,1)S(1)}, u32[]{:S(2)}, u32[]{:S(2)}) collective-permute-start(bf16[256,256]{1,0:T(8,128)(2,1)S(1)} %get-tuple-element.39), channel_id=1, source_target_pairs={{0,2},{2,0},{4,6},{6,4},{1,3},{3,1},{5,7},{7,5},{8,10},{10,8},{12,... | collective-permute-start | bytes 393224 | tf_op jit(solution)/shard_map/ppermute | solution.py:317
  5.9 2.6 %collective-permute-start.2 = (bf16[256,256]{1,0:T(8,128)(2,1)S(1)}, bf16[256,256]{1,0:T(8,128)(2,1)S(1)}, u32[]{:S(2)}, u32[]{:S(2)}) collective-permute-start(bf16[256,256]{1,0:T(8,128)(2,1)S(1)} %get-tuple-element.40), channel_id=1, source_target_pairs={{0,4},{2,6},{4,0},{6,2},{1,5},{3,7},{5,1},{7,3},{8,12},{10,14},{12... | collective-permute-start | bytes 393224 | tf_op jit(solution)/shard_map/ppermute | solution.py:317
  8.6 1.9 %shard_map.115 = (bf16[256,128]{1,0:T(8,128)(2,1)S(1)}, bf16[256,128]{1,0:T(8,128)(2,1)S(1)}, bf16[256,128]{1,0:T(8,128)(2,1)S(1)}, bf16[256,128]{1,0:T(8,128)(2,1)S(1)}, bf16[256,256]{1,0:T(8,128)(2,1)S(1)}) custom-call(bf16[256,1024]{1,0:T(8,128)(2,1)S(1)} %get-tuple-element.33.normed, bf16[1024,1024]{1,0:T(8,128)(2,1)S(1)} %copy-done, ...), custom_call_target="tpu_custom_call" | custom-call | flops 268435456 | bytes 4194304 | tf_op jit(solution)/shard_map/pallas_call | solution.py:346
  10.5 4.4 %collective-permute-done.2.refs_2_ = bf16[256,256]{1,0:T(8,128)(2,1)S(1)} collective-permute-done((bf16[256,256]{1,0:T(8,128)(2,1)S(1)}, bf16[256,256]{1,0:T(8,128)(2,1)S(1)}, u32[]{:S(2)}, u32[]{:S(2)}) %collective-permute-start.2) | collective-permute-done | bytes 131104 | tf_op jit(solution)/shard_map/ppermute | solution.py:317
  14.9 2.5 %collective-permute-done.3.refs_3_ = bf16[256,256]{1,0:T(8,128)(2,1)S(1)} collective-permute-done((bf16[256,256]{1,0:T(8,128)(2,1)S(1)}, bf16[256,256]{1,0:T(8,128)(2,1)S(1)}, u32[]{:S(2)}, u32[]{:S(2)}) %collective-permute-start.3) | collective-permute-done | bytes 131104 | tf_op jit(solution)/shard_map/ppermute | solution.py:317
  17.5 2.1 %shard_map.116 = (bf16[520,128]{1,0:T(8,128)(2,1)S(1)}, bf16[520,128]{1,0:T(8,128)(2,1)S(1)}, f32[2,128,1024]{2,1,0:T(8,128)S(1)}, bf16[2048,128]{1,0:T(8,128)(2,1)S(1)}) custom-call(bf16[256,256]{1,0:T(8,128)(2,1)S(1)} %get-tuple-element.38.refs_0_, bf16[256,256]{1,0:T(8,128)(2,1)S(1)} %collective-permute-done.1.refs_1_, ...), custom_call_target="tpu_custom_call" | custom-call | flops 1090519040 | bytes 2097152 | tf_op jit(solution)/shard_map/pallas_call | solution.py:357
  20.5 3.8 %collective-permute-start.9 = (bf16[520,128]{1,0:T(8,128)(2,1)S(1)}, bf16[520,128]{1,0:T(8,128)(2,1)S(1)}, u32[]{:S(2)}, u32[]{:S(2)}) collective-permute-start(bf16[520,128]{1,0:T(8,128)(2,1)S(1)} %shard_map.117.after), channel_id=1, source_target_pairs={{0,24},{8,16},{16,8},{24,0},{1,25},{9,17},{17,9},{25,1},{2,26},{10... | collective-permute-start | bytes 399368 | tf_op jit(solution)/shard_map/ppermute | solution.py:372
  24.4 1.3 %collective-permute-start.8 = (bf16[520,128]{1,0:T(8,128)(2,1)S(1)}, bf16[520,128]{1,0:T(8,128)(2,1)S(1)}, u32[]{:S(2)}, u32[]{:S(2)}) collective-permute-start(bf16[520,128]{1,0:T(8,128)(2,1)S(1)} %get-tuple-element.49), channel_id=1, source_target_pairs={{0,16},{8,24},{16,0},{24,8},{1,17},{9,25},{17,1},{25,9},{2,18},{10... | collective-permute-start | bytes 399368 | tf_op jit(solution)/shard_map/ppermute | solution.py:372
  25.6 1.2 %collective-permute-start.5 = (bf16[256,128]{1,0:T(8,128)(2,1)S(1)}, bf16[256,128]{1,0:T(8,128)(2,1)S(1)}, u32[]{:S(2)}, u32[]{:S(2)}) collective-permute-start(bf16[256,128]{1,0:T(8,128)(2,1)S(1)} %get-tuple-element.46), channel_id=1, source_target_pairs={{0,4},{2,6},{4,0},{6,2},{1,5},{3,7},{5,1},{7,3},{8,12},{10,14},{12... | collective-permute-start | bytes 196616 | tf_op jit(solution)/shard_map/ppermute | solution.py:317
  27.4 2.1 %collective-permute-start.6 = (bf16[256,128]{1,0:T(8,128)(2,1)S(1)}, bf16[256,128]{1,0:T(8,128)(2,1)S(1)}, u32[]{:S(2)}, u32[]{:S(2)}) collective-permute-start(bf16[256,128]{1,0:T(8,128)(2,1)S(1)} %get-tuple-element.47), channel_id=1, source_target_pairs={{0,6},{2,4},{4,2},{6,0},{1,7},{3,5},{5,3},{7,1},{8,14},{10,12},{12... | collective-permute-start | bytes 196616 | tf_op jit(solution)/shard_map/ppermute | solution.py:317
  31.5 2.5 %collective-permute-start.12 = (bf16[520,128]{1,0:T(8,128)(2,1)S(1)}, bf16[520,128]{1,0:T(8,128)(2,1)S(1)}, u32[]{:S(2)}, u32[]{:S(2)}) collective-permute-start(bf16[520,128]{1,0:T(8,128)(2,1)S(1)} %shard_map.120.refs_4_), channel_id=1, source_target_pairs={{0,96},{32,64},{64,32},{96,0},{1,97},{33,65},{65,33},{97,1},{2,98}... | collective-permute-start | bytes 399368 | tf_op jit(solution)/shard_map/ppermute | solution.py:386
  34.9 2.2 %shard_map.118.refs_8_.refs_0_.phi = bf16[2080,2048]{1,0:T(8,128)(2,1)S(1)} custom-call(bf16[256,128]{1,0:T(8,128)(2,1)S(1)} %get-tuple-element.44.refs_0_.refs_4_, bf16[256,128]{1,0:T(8,128)(2,1)S(1)} %collective-permute-done.4.refs_1_.refs_5_, bf16[256,128]{1,0:T(8,128)(2,1)S(1)} %collective-permute-done.5.refs_2_.refs_6_, ...), custom_call_target="tpu_custom_call" | custom-call | flops 545259520 | bytes 9437184 | tf_op jit(solution)/shard_map/pallas_call | solution.py:388
  37.0 2.1 %shard_map.121.refs_9_.refs_5_.inside = f32[1024,128]{1,0:T(8,128)S(1)} custom-call(bf16[256,256]{1,0:T(8,128)(2,1)S(1)} %get-tuple-element.38.refs_0_, bf16[256,256]{1,0:T(8,128)(2,1)S(1)} %collective-permute-done.1.refs_1_, bf16[256,256]{1,0:T(8,128)(2,1)S(1)} %collective-permute-done.2.refs_2_, bf16[256,256]{1,0:T(8,128)(2,1)S(1)} %collective-permute-done.3.refs_3_, ...), custom_call_target="tpu_custom_call" | custom-call | flops 1073741824 | bytes 2097152 | tf_op jit(solution)/shard_map/pallas_call | solution.py:375
  40.1 3.0 %collective-permute-start.14 = (bf16[520,128]{1,0:T(8,128)(2,1)S(1)}, bf16[520,128]{1,0:T(8,128)(2,1)S(1)}, u32[]{:S(2)}, u32[]{:S(2)}) collective-permute-start(bf16[520,128]{1,0:T(8,128)(2,1)S(1)} %get-tuple-element.52), channel_id=1, source_target_pairs={{0,16},{8,24},{16,0},{24,8},{1,17},{9,25},{17,1},{25,9},{2,18},{10... | collective-permute-start | bytes 399368 | tf_op jit(solution)/shard_map/ppermute | solution.py:317
  44.0 2.9 %collective-permute-done.14.refs_3_ = bf16[520,128]{1,0:T(8,128)(2,1)S(1)} collective-permute-done((bf16[520,128]{1,0:T(8,128)(2,1)S(1)}, bf16[520,128]{1,0:T(8,128)(2,1)S(1)}, u32[]{:S(2)}, u32[]{:S(2)}) %collective-permute-start.14) | collective-permute-done | bytes 133152 | tf_op jit(solution)/shard_map/ppermute | solution.py:317
  46.9 1.4 %collective-permute-done.15.refs_4_ = bf16[520,128]{1,0:T(8,128)(2,1)S(1)} collective-permute-done((bf16[520,128]{1,0:T(8,128)(2,1)S(1)}, bf16[520,128]{1,0:T(8,128)(2,1)S(1)}, u32[]{:S(2)}, u32[]{:S(2)}) %collective-permute-start.15) | collective-permute-done | bytes 133152 | tf_op jit(solution)/shard_map/ppermute | solution.py:317
  48.3 1.7 %shard_map.123 = (bf16[256,128]{1,0:T(8,128)(2,1)S(1)}, bf16[256,128]{1,0:T(8,128)(2,1)S(1)}, bf16[256,128]{1,0:T(8,128)(2,1)S(1)}, bf16[128,2080]{1,0:T(8,128)(2,1)S(1)}) custom-call(bf16[2080,2048]{1,0:T(8,128)(2,1)S(1)} %shard_map.118.refs_8_.refs_0_.phi, bf16[520,128]{1,0:T(8,128)(2,1)S(1)} %get-tuple-element.50.refs_1_, ...), custom_call_target="tpu_custom_call" | custom-call | flops 1635778560 | bytes 2097152 | tf_op jit(solution)/shard_map/pallas_call | solution.py:403
  50.1 1.4 %collective-permute-start.17 = (bf16[256,128]{1,0:T(8,128)(2,1)S(1)}, bf16[256,128]{1,0:T(8,128)(2,1)S(1)}, u32[]{:S(2)}, u32[]{:S(2)}) collective-permute-start(bf16[256,128]{1,0:T(8,128)(2,1)S(1)} %get-tuple-element.56), channel_id=1, source_target_pairs={{0,4},{2,6},{4,0},{6,2},{1,5},{3,7},{5,1},{7,3},{8,12},{10,14},{12... | collective-permute-start | bytes 196616 | tf_op jit(solution)/shard_map/ppermute | solution.py:412
  51.5 2.4 %collective-permute-start.18 = (bf16[256,128]{1,0:T(8,128)(2,1)S(1)}, bf16[256,128]{1,0:T(8,128)(2,1)S(1)}, u32[]{:S(2)}, u32[]{:S(2)}) collective-permute-start(bf16[256,128]{1,0:T(8,128)(2,1)S(1)} %get-tuple-element.57), channel_id=1, source_target_pairs={{0,6},{2,4},{4,2},{6,0},{1,7},{3,5},{5,3},{7,1},{8,14},{10,12},{12... | collective-permute-start | bytes 196616 | tf_op jit(solution)/shard_map/ppermute | solution.py:412
  54.8 1.0 %collective-permute-done.18.refs_3_ = bf16[256,128]{1,0:T(8,128)(2,1)S(1)} collective-permute-done((bf16[256,128]{1,0:T(8,128)(2,1)S(1)}, bf16[256,128]{1,0:T(8,128)(2,1)S(1)}, u32[]{:S(2)}, u32[]{:S(2)}) %collective-permute-start.18) | collective-permute-done | bytes 65568 | tf_op jit(solution)/shard_map/ppermute | solution.py:412
  55.9 7.0 %collective-permute-start.19 = (bf16[128,512]{1,0:T(8,128)(2,1)S(1)}, bf16[128,512]{1,0:T(8,128)(2,1)S(1)}, u32[]{:S(2)}, u32[]{:S(2)}) collective-permute-start(bf16[128,512]{1,0:T(8,128)(2,1)S(1)} %shard_map.125), channel_id=1, source_target_pairs={{0,1},{1,0},{2,3},{3,2},{4,5},{5,4},{6,7},{7,6},{8,9},{9,8},{10,11... | collective-permute-start | bytes 393224 | tf_op jit(solution)/shard_map/ppermute | solution.py:418
  63.9 4.0 %shard_map.126 = (bf16[128,1024]{1,0:T(8,128)(2,1)}, bf16[128,1024]{1,0:T(8,128)(2,1)}) custom-call(bf16[256,128]{1,0:T(8,128)(2,1)S(1)} %shard_map.124.refs_0_, bf16[256,128]{1,0:T(8,128)(2,1)S(1)} %collective-permute-done.16.refs_1_, bf16[256,128]{1,0:T(8,128)(2,1)S(1)} %collective-permute-done.17.refs_2_, ...), custom_call_target="tpu_custom_call" | custom-call | flops 2415919104 | bytes 18874368 | tf_op jit(solution)/shard_map/pallas_call | solution.py:420
  (50 shorter events, 8.9 us)
Async XLA Ops:
  0.6 3.1 %collective-permute-start = (bf16[128,1024]{1,0:T(8,128)(2,1)}, bf16[128,1024]{1,0:T(8,128)(2,1)S(1)}, u32[]{:S(2)}, u32[]{:S(2)}) collective-permute-start(bf16[128,1024]{1,0:T(8,128)(2,1)} %refs_5_.1), channel_id=1, source_target_pairs={{0,1},{1,0},{2,3},{3,2},{4,5},{5,4},{6,7},{7,6},{8,9},{9,8},{10,11... | collective-permute-start | bytes 786440 | tf_op jit(solution)/shard_map/ppermute | solution.py:322
  4.4 6.0 %collective-permute-start.1 = (bf16[256,256]{1,0:T(8,128)(2,1)S(1)}, bf16[256,256]{1,0:T(8,128)(2,1)S(1)}, u32[]{:S(2)}, u32[]{:S(2)}) collective-permute-start(bf16[256,256]{1,0:T(8,128)(2,1)S(1)} %get-tuple-element.39), channel_id=1, source_target_pairs={{0,2},{2,0},{4,6},{6,4},{1,3},{3,1},{5,7},{7,5},{8,10},{10,8},{12,... | collective-permute-start | bytes 393224 | tf_op jit(solution)/shard_map/ppermute | solution.py:317
  5.9 9.0 %collective-permute-start.2 = (bf16[256,256]{1,0:T(8,128)(2,1)S(1)}, bf16[256,256]{1,0:T(8,128)(2,1)S(1)}, u32[]{:S(2)}, u32[]{:S(2)}) collective-permute-start(bf16[256,256]{1,0:T(8,128)(2,1)S(1)} %get-tuple-element.40), channel_id=1, source_target_pairs={{0,4},{2,6},{4,0},{6,2},{1,5},{3,7},{5,1},{7,3},{8,12},{10,14},{12... | collective-permute-start | bytes 393224 | tf_op jit(solution)/shard_map/ppermute | solution.py:317
  8.6 8.9 %collective-permute-start.3 = (bf16[256,256]{1,0:T(8,128)(2,1)S(1)}, bf16[256,256]{1,0:T(8,128)(2,1)S(1)}, u32[]{:S(2)}, u32[]{:S(2)}) collective-permute-start(bf16[256,256]{1,0:T(8,128)(2,1)S(1)} %get-tuple-element.41), channel_id=1, source_target_pairs={{0,6},{2,4},{4,2},{6,0},{1,7},{3,5},{5,3},{7,1},{8,14},{10,12},{12... | collective-permute-start | bytes 393224 | tf_op jit(solution)/shard_map/ppermute | solution.py:317
  20.5 6.9 %collective-permute-start.9 = (bf16[520,128]{1,0:T(8,128)(2,1)S(1)}, bf16[520,128]{1,0:T(8,128)(2,1)S(1)}, u32[]{:S(2)}, u32[]{:S(2)}) collective-permute-start(bf16[520,128]{1,0:T(8,128)(2,1)S(1)} %shard_map.117.after), channel_id=1, source_target_pairs={{0,24},{8,16},{16,8},{24,0},{1,25},{9,17},{17,9},{25,1},{2,26},{10... | collective-permute-start | bytes 399368 | tf_op jit(solution)/shard_map/ppermute | solution.py:372
  24.4 6.1 %collective-permute-start.7 = (bf16[520,128]{1,0:T(8,128)(2,1)S(1)}, bf16[520,128]{1,0:T(8,128)(2,1)S(1)}, u32[]{:S(2)}, u32[]{:S(2)}) collective-permute-start(bf16[520,128]{1,0:T(8,128)(2,1)S(1)} %get-tuple-element.48), channel_id=1, source_target_pairs={{0,8},{8,0},{16,24},{24,16},{1,9},{9,1},{17,25},{25,17},{2,10},{10... | collective-permute-start | bytes 399368 | tf_op jit(solution)/shard_map/ppermute | solution.py:372
  24.4 7.1 %collective-permute-start.8 = (bf16[520,128]{1,0:T(8,128)(2,1)S(1)}, bf16[520,128]{1,0:T(8,128)(2,1)S(1)}, u32[]{:S(2)}, u32[]{:S(2)}) collective-permute-start(bf16[520,128]{1,0:T(8,128)(2,1)S(1)} %get-tuple-element.49), channel_id=1, source_target_pairs={{0,16},{8,24},{16,0},{24,8},{1,17},{9,25},{17,1},{25,9},{2,18},{10... | collective-permute-start | bytes 399368 | tf_op jit(solution)/shard_map/ppermute | solution.py:372
  25.6 9.0 %collective-permute-start.4 = (bf16[256,128]{1,0:T(8,128)(2,1)S(1)}, bf16[256,128]{1,0:T(8,128)(2,1)S(1)}, u32[]{:S(2)}, u32[]{:S(2)}) collective-permute-start(bf16[256,128]{1,0:T(8,128)(2,1)S(1)} %get-tuple-element.45), channel_id=1, source_target_pairs={{0,2},{2,0},{4,6},{6,4},{1,3},{3,1},{5,7},{7,5},{8,10},{10,8},{12,... | collective-permute-start | bytes 196616 | tf_op jit(solution)/shard_map/ppermute | solution.py:317
  25.6 9.2 %collective-permute-start.5 = (bf16[256,128]{1,0:T(8,128)(2,1)S(1)}, bf16[256,128]{1,0:T(8,128)(2,1)S(1)}, u32[]{:S(2)}, u32[]{:S(2)}) collective-permute-start(bf16[256,128]{1,0:T(8,128)(2,1)S(1)} %get-tuple-element.46), channel_id=1, source_target_pairs={{0,4},{2,6},{4,0},{6,2},{1,5},{3,7},{5,1},{7,3},{8,12},{10,14},{12... | collective-permute-start | bytes 196616 | tf_op jit(solution)/shard_map/ppermute | solution.py:317
  27.4 7.4 %collective-permute-start.6 = (bf16[256,128]{1,0:T(8,128)(2,1)S(1)}, bf16[256,128]{1,0:T(8,128)(2,1)S(1)}, u32[]{:S(2)}, u32[]{:S(2)}) collective-permute-start(bf16[256,128]{1,0:T(8,128)(2,1)S(1)} %get-tuple-element.47), channel_id=1, source_target_pairs={{0,6},{2,4},{4,2},{6,0},{1,7},{3,5},{5,3},{7,1},{8,14},{10,12},{12... | collective-permute-start | bytes 196616 | tf_op jit(solution)/shard_map/ppermute | solution.py:317
  31.5 7.6 %collective-permute-start.12 = (bf16[520,128]{1,0:T(8,128)(2,1)S(1)}, bf16[520,128]{1,0:T(8,128)(2,1)S(1)}, u32[]{:S(2)}, u32[]{:S(2)}) collective-permute-start(bf16[520,128]{1,0:T(8,128)(2,1)S(1)} %shard_map.120.refs_4_), channel_id=1, source_target_pairs={{0,96},{32,64},{64,32},{96,0},{1,97},{33,65},{65,33},{97,1},{2,98}... | collective-permute-start | bytes 399368 | tf_op jit(solution)/shard_map/ppermute | solution.py:386
  34.1 5.4 %collective-permute-start.11 = (bf16[520,128]{1,0:T(8,128)(2,1)S(1)}, bf16[520,128]{1,0:T(8,128)(2,1)S(1)}, u32[]{:S(2)}, u32[]{:S(2)}) collective-permute-start(bf16[520,128]{1,0:T(8,128)(2,1)S(1)} %shard_map.120.refs_4_), channel_id=1, source_target_pairs={{0,64},{32,96},{64,0},{96,32},{1,65},{33,97},{65,1},{97,33},{2,66}... | collective-permute-start | bytes 399368 | tf_op jit(solution)/shard_map/ppermute | solution.py:386
  34.6 5.0 %collective-permute-start.10 = (bf16[520,128]{1,0:T(8,128)(2,1)S(1)}, bf16[520,128]{1,0:T(8,128)(2,1)S(1)}, u32[]{:S(2)}, u32[]{:S(2)}) collective-permute-start(bf16[520,128]{1,0:T(8,128)(2,1)S(1)} %shard_map.120.refs_4_), channel_id=1, source_target_pairs={{0,32},{32,0},{64,96},{96,64},{1,33},{33,1},{65,97},{97,65},{2,34}... | collective-permute-start | bytes 399368 | tf_op jit(solution)/shard_map/ppermute | solution.py:386
  39.6 24.3 %slice-start.2 = ((s8[8388608]{0:T(1024)(128)(4,1)}), s8[4194304]{0:T(1024)(128)(4,1)S(1)}, s32[]{:S(2)}) async-start(s8[8388608]{0:T(1024)(128)(4,1)} %bitcast.5), calls=%async_computation.2 | async-start | bytes 8388608
  40.0 3.9 %collective-permute-start.13 = (bf16[520,128]{1,0:T(8,128)(2,1)S(1)}, bf16[520,128]{1,0:T(8,128)(2,1)S(1)}, u32[]{:S(2)}, u32[]{:S(2)}) collective-permute-start(bf16[520,128]{1,0:T(8,128)(2,1)S(1)} %get-tuple-element.51), channel_id=1, source_target_pairs={{0,8},{8,0},{16,24},{24,16},{1,9},{9,1},{17,25},{25,17},{2,10},{10... | collective-permute-start | bytes 399368 | tf_op jit(solution)/shard_map/ppermute | solution.py:317
  40.1 6.8 %collective-permute-start.14 = (bf16[520,128]{1,0:T(8,128)(2,1)S(1)}, bf16[520,128]{1,0:T(8,128)(2,1)S(1)}, u32[]{:S(2)}, u32[]{:S(2)}) collective-permute-start(bf16[520,128]{1,0:T(8,128)(2,1)S(1)} %get-tuple-element.52), channel_id=1, source_target_pairs={{0,16},{8,24},{16,0},{24,8},{1,17},{9,25},{17,1},{25,9},{2,18},{10... | collective-permute-start | bytes 399368 | tf_op jit(solution)/shard_map/ppermute | solution.py:317
  43.1 5.2 %collective-permute-start.15 = (bf16[520,128]{1,0:T(8,128)(2,1)S(1)}, bf16[520,128]{1,0:T(8,128)(2,1)S(1)}, u32[]{:S(2)}, u32[]{:S(2)}) collective-permute-start(bf16[520,128]{1,0:T(8,128)(2,1)S(1)} %get-tuple-element.53), channel_id=1, source_target_pairs={{0,24},{8,16},{16,8},{24,0},{1,25},{9,17},{17,9},{25,1},{2,26},{10... | collective-permute-start | bytes 399368 | tf_op jit(solution)/shard_map/ppermute | solution.py:317
  48.3 15.6 %slice-start = ((s8[8388608]{0:T(1024)(128)(4,1)}), s8[4194304]{0:T(1024)(128)(4,1)S(1)}, s32[]{:S(2)}) async-start(s8[8388608]{0:T(1024)(128)(4,1)} %bitcast.3), calls=%async_computation | async-start | bytes 8388608
  48.3 15.6 %slice-start.3 = ((s8[8388608]{0:T(1024)(128)(4,1)}), s8[4194304]{0:T(1024)(128)(4,1)S(1)}, s32[]{:S(2)}) async-start(s8[8388608]{0:T(1024)(128)(4,1)} %bitcast.5), calls=%async_computation.3 | async-start | bytes 8388608
  50.0 4.7 %collective-permute-start.16 = (bf16[256,128]{1,0:T(8,128)(2,1)S(1)}, bf16[256,128]{1,0:T(8,128)(2,1)S(1)}, u32[]{:S(2)}, u32[]{:S(2)}) collective-permute-start(bf16[256,128]{1,0:T(8,128)(2,1)S(1)} %get-tuple-element.55), channel_id=1, source_target_pairs={{0,2},{2,0},{4,6},{6,4},{1,3},{3,1},{5,7},{7,5},{8,10},{10,8},{12,... | collective-permute-start | bytes 196616 | tf_op jit(solution)/shard_map/ppermute | solution.py:412
  50.1 4.7 %collective-permute-start.17 = (bf16[256,128]{1,0:T(8,128)(2,1)S(1)}, bf16[256,128]{1,0:T(8,128)(2,1)S(1)}, u32[]{:S(2)}, u32[]{:S(2)}) collective-permute-start(bf16[256,128]{1,0:T(8,128)(2,1)S(1)} %get-tuple-element.56), channel_id=1, source_target_pairs={{0,4},{2,6},{4,0},{6,2},{1,5},{3,7},{5,1},{7,3},{8,12},{10,14},{12... | collective-permute-start | bytes 196616 | tf_op jit(solution)/shard_map/ppermute | solution.py:412
  51.5 4.3 %collective-permute-start.18 = (bf16[256,128]{1,0:T(8,128)(2,1)S(1)}, bf16[256,128]{1,0:T(8,128)(2,1)S(1)}, u32[]{:S(2)}, u32[]{:S(2)}) collective-permute-start(bf16[256,128]{1,0:T(8,128)(2,1)S(1)} %get-tuple-element.57), channel_id=1, source_target_pairs={{0,6},{2,4},{4,2},{6,0},{1,7},{3,5},{5,3},{7,1},{8,14},{10,12},{12... | collective-permute-start | bytes 196616 | tf_op jit(solution)/shard_map/ppermute | solution.py:412
  54.0 9.9 %copy-start.3 = (f32[1024]{0:T(1024)S(1)}, f32[1024]{0:T(1024)}, u32[]{:S(2)}) copy-start(f32[1024]{0:T(1024)} %param.17) | copy-start | bytes 12292
  55.9 8.0 %collective-permute-start.19 = (bf16[128,512]{1,0:T(8,128)(2,1)S(1)}, bf16[128,512]{1,0:T(8,128)(2,1)S(1)}, u32[]{:S(2)}, u32[]{:S(2)}) collective-permute-start(bf16[128,512]{1,0:T(8,128)(2,1)S(1)} %shard_map.125), channel_id=1, source_target_pairs={{0,1},{1,0},{2,3},{3,2},{4,5},{5,4},{6,7},{7,6},{8,9},{9,8},{10,11... | collective-permute-start | bytes 393224 | tf_op jit(solution)/shard_map/ppermute | solution.py:418
  (5 other events, 43.8 us)
where the time goes:
time: 68.1 us; the launch traced here: 67.9 us
  starting transfers between devices  32.2 us (47%)
  Pallas kernels  19.4 us (28%)
  waiting for transfers between devices  15.4 us (23%)
  between operations  0.84 us (1%)
    ppermute x9, starting transfers between devices, exchange(): moved = {k: lax.ppermute(parts[k], axis, xor_pairs(4, k)) for k in ORDER}  11.3 us
    ppermute x9, waiting for transfers between devices, exchange(): moved = {k: lax.ppermute(parts[k], axis, xor_pairs(4, k)) for k in ORDER}  11.3 us
    ppermute x1, starting transfers between devices, body(): other = lax.ppermute(other, 'c', xor_pairs(2, 1))  7 us
    ppermute x3, starting transfers between devices, body(): pieces.append(lax.ppermute(piece, 'z', xor_pairs(4, k)))  5.12 us
    pallas_call x1, Pallas kernels, body(): call(mlp_kernel, [arr(ROWS, D)] * 2, [], [VM] * 10, 8, flops=2 * 128 * 10...  3.96 us
    ppermute x3, starting transfers between devices, body(): moved = {k: lax.ppermute(parts[k - 1], 'y', xor_pairs(4, k)) for k in ORDER}  3.93 us
    ppermute x3, starting transfers between devices, body(): moved = {k: lax.ppermute(total, 'x', xor_pairs(4, k)) for k in ORDER}  3.33 us
    pallas_call x1, Pallas kernels, body(): call(features_kernel, arr(NF, 2 * LEN), [pltpu.VMEM((2, 2 * HS, LEN), F32...  2.16 us
  transfers between devices with their start and end apart: 20, of which 11 were waited for; matrix products, arithmetic and copies ran while one was open for 0% of the time, Pallas kernels for 14%

commit v1 on v0

--- a/solution.py
+++ b/solution.py
@@ -99,26 +99,29 @@
 
 def fill_queries(ext, h, phi, col):
     for d in range(32):
-        row = MAIN * (d % 4) + HS * (d // 4)
-        phi[row : row + HS, col : col + LEN] = (ext[h, 0:HS, :] * ext[h, d : d + HS, :]).astype(BF)
+        phi[d * HS : (d + 1) * HS, col : col + LEN] = (
+            ext[h, 0:HS, :] * ext[h, d : d + HS, :]
+        ).astype(BF)
     phi[4 * MAIN : NF, col : col + LEN] = (ext[h, 0:32, :] * ext[h, 32:HS, :]).astype(BF)
 
 
 def key_piece(ext, vz, phi, turned, k):
     c = flip(lax.axis_index("z"), k)
+    total = None
     for h in range(2):
-        col = slice(h * LEN, (h + 1) * LEN)
-        turned[...] = pltpu.roll(ext[h], lax.rem(2 * HS - c, 2 * HS), 0)
+        turned[h] = ext[h, pl.ds(pl.multiple_of(8 * c, 8), HS + 8), :]
         for j in range(8):
             left = ext[h, 0:HS, :]
             twice = left + left
             if j == 0:
                 twice = jnp.where(c == 0, left, twice)
-            phi[j * HS : (j + 1) * HS, col] = (twice * turned[4 * j : 4 * j + HS, :]).astype(BF)
+            phi[h, j * HS : (j + 1) * HS, :] = (twice * turned[h, j : j + HS, :]).astype(BF)
         low = ext[h, pl.ds(pl.multiple_of(8 * c, 8), 8), :]
         high = ext[h, pl.ds(pl.multiple_of(8 * c + 32, 8), 8), :]
-        phi[MAIN:PIECE, col] = ((low + low) * high).astype(BF)
-    return jnp.dot(phi[...], vz[...], preferred_element_type=F32).astype(BF)
+        phi[h, MAIN:PIECE, :] = ((low + low) * high).astype(BF)
+        part = jnp.dot(phi[h], vz[h * LEN : (h + 1) * LEN], preferred_element_type=F32)
+        total = part if total is None else total + part
+    return total.astype(BF)
 
 
 def state_kernel(*refs):
@@ -136,8 +139,8 @@
             ext[h, HS : 2 * HS, at] = part
             mine = (lane >= HS) if h else (lane < HS)
             vz[h * LEN + k * PAIR : h * LEN + (k + 1) * PAIR, :] = jnp.where(mine, value, zero)
-    for out, k in zip(outs, (1, 2)):
-        out[...] = key_piece(ext, vz, phi, turned, k)
+    for i, (out, k) in enumerate(zip(outs, (1, 2))):
+        out[...] = key_piece(ext, vz, phi.at[i], turned.at[i], k)
 
 
 def third_kernel(ext, vz, out, phi, turned):
@@ -274,10 +277,10 @@
     y, c = lax.axis_index("y"), lax.axis_index("c")
     row = pl.multiple_of(c * ROWS, ROWS)
     for k in range(4):
-        col = pl.multiple_of((2 * flip(y, k) + c) * 128, 128)
-        att[:, pl.ds(col, 128)] = parts[k][pl.ds(row, ROWS), :]
-        col = pl.multiple_of((2 * k + 1 - c) * 128, 128)
-        att[:, pl.ds(col, 128)] = other[:, k * 128 : (k + 1) * 128]
+        col = 2 * flip(y, k) + ((1 - c) if k else c)
+        att[:, pl.ds(pl.multiple_of(col * 128, 128), 128)] = parts[k][pl.ds(row, ROWS), :]
+        col = 2 * k + jnp.where(y == k, 1 - c, c)
+        att[:, pl.ds(pl.multiple_of(col * 128, 128), 128)] = other[:, k * 128 : (k + 1) * 128]
     stream = tok[...].astype(F32) + jnp.dot(att[...], wo[...], preferred_element_type=F32)
     stream = stream.astype(BF).astype(F32)
     normed = rms(stream, gain[...]).astype(BF)
@@ -352,14 +355,15 @@
         flops=2 * 256 * 1024 * 512,
         moved=4 * MIB,
     )(normed, w_query, fixed(w_key), fixed(w_value))
-    spare = [pltpu.VMEM((PIECE, 2 * LEN), BF), pltpu.VMEM((2 * HS, LEN), F32)]
+    spare = [pltpu.VMEM((2, PIECE, LEN), BF), pltpu.VMEM((2, HS + 8, LEN), F32)]
+    twice = [pltpu.VMEM((2, 2, PIECE, LEN), BF), pltpu.VMEM((2, 2, HS + 8, LEN), F32)]
     cost = 2 * PIECE * 2 * LEN * 256
     first, second, ext, vz = call(
         state_kernel,
         [arr(PIECE, 128)] * 2 + [arr(2, 2 * HS, LEN, dtype=F32), arr(2 * LEN, 128)],
-        spare,
+        twice,
         [VM] * 4,
-        8,
+        12,
         flops=2 * cost,
         moved=2 * MIB,
     )(*pairs)
@@ -409,7 +413,8 @@
         flops=2 * NF * 2 * LEN * 192,
         moved=2 * MIB,
     )(phi, *states, inside, scale)
-    moved = {k: lax.ppermute(parts[k - 1], "y", xor_pairs(4, k)) for k in ORDER}
+    swaps = {k: [(i, i ^ (2 * k + 1)) for i in range(8)] for k in ORDER}
+    moved = {k: lax.ppermute(parts[k - 1], ("y", "c"), swaps[k]) for k in ORDER}
     mine = call(
         own_kernel, arr(PAIR, 128), [], [VM] * 4, 8, flops=2 * NF * 2 * LEN * 64, moved=2 * MIB
     )(phi, turned, inside, scale)

time: 68.1 us -> 67 us (0.984)
  starting transfers between devices: 32.2 us -> 30.9 us
  waiting for transfers between devices: 15.4 us -> 16.3 us
  Pallas kernels: 19.4 us -> 18.7 us
    ppermute x1, starting transfers between devices: 7 us -> 0.47 us  [body(): other = lax.ppermute(other, 'c', xor_pairs(2, 1))]
    ppermute x3, starting transfers between devices: 3.93 us -> 9.23 us  [body(): moved = {k: lax.ppermute(parts[k - 1], ('y', 'c'), swaps[k]) for k in ORDER}]
    ppermute x3, waiting for transfers between devices: 1.14 us -> 1.89 us  [body(): moved = {k: lax.ppermute(parts[k - 1], ('y', 'c'), swaps[k]) for k in ORDER}]
  transfers between devices with their start and end apart: 20 -> 20, of which waited for: 11 -> 10; matrix products, arithmetic and copies ran while one was open for 0% -> 0% of each run, Pallas kernels for 14% -> 14%
where the time goes in v1:
time: 67 us; the launch traced here: 66.9 us
  starting transfers between devices  30.9 us (46%)
  Pallas kernels  18.7 us (28%)
  waiting for transfers between devices  16.3 us (24%)
  between operations  0.84 us (1%)
    ppermute x9, starting transfers between devices, exchange(): moved = {k: lax.ppermute(parts[k], axis, xor_pairs(4, k)) for k in ORDER}  11.3 us
    ppermute x9, waiting for transfers between devices, exchange(): moved = {k: lax.ppermute(parts[k], axis, xor_pairs(4, k)) for k in ORDER}  11.3 us
    ppermute x3, starting transfers between devices, body(): moved = {k: lax.ppermute(parts[k - 1], ('y', 'c'), swaps[k]) for k in ORDER}  9.23 us
    ppermute x3, starting transfers between devices, body(): pieces.append(lax.ppermute(piece, 'z', xor_pairs(4, k)))  5.11 us
    pallas_call x1, Pallas kernels, body(): call(mlp_kernel, [arr(ROWS, D)] * 2, [], [VM] * 10, 8, flops=2 * 128 * 10...  3.96 us
    ppermute x3, starting transfers between devices, body(): moved = {k: lax.ppermute(total, 'x', xor_pairs(4, k)) for k in ORDER}  3.33 us
    pallas_call x1, Pallas kernels, body(): call(features_kernel, arr(NF, 2 * LEN), [pltpu.VMEM((2, 2 * HS, LEN), F32...  2.16 us
    pallas_call x1, Pallas kernels, body(): call(inside_kernel, arr(LEN, 128, dtype=F32), [pltpu.VMEM((LEN, 128), BF)...  2.08 us
  transfers between devices with their start and end apart: 20, of which 10 were waited for; matrix products, arithmetic and copies ran while one was open for 0% of the time, Pallas kernels for 14%

profile of v1, /device:TPU:1, one launch (start us, length us, event | category | flops | bytes accessed | tf_op | source)
XLA Modules:
  0.0 66.9 jit_solution(17880522860439096970)
XLA Ops:
  0.6 1.5 %collective-permute-start = (bf16[128,1024]{1,0:T(8,128)(2,1)}, bf16[128,1024]{1,0:T(8,128)(2,1)S(1)}, u32[]{:S(2)}, u32[]{:S(2)}) collective-permute-start(bf16[128,1024]{1,0:T(8,128)(2,1)} %refs_5_.1), channel_id=1, source_target_pairs={{0,1},{1,0},{2,3},{3,2},{4,5},{5,4},{6,7},{7,6},{8,9},{9,8},{10,11... | collective-permute-start | bytes 786440 | tf_op jit(solution)/shard_map/ppermute | solution.py:325
  2.1 1.6 %shard_map.113 = (bf16[128,1024]{1,0:T(8,128)(2,1)S(1)}, f32[1,1024]{1,0:T(1,128)S(1)}, bf16[3,1024,256]{2,1,0:T(8,128)(2,1)S(1)}) custom-call(bf16[128,1024]{1,0:T(8,128)(2,1)} %refs_5_.1, f32[1,1024]{1,0:T(1,128)} %bitcast.10, bf16[1024,1024]{1,0:T(8,128)(2,1)} %wk.3, bf16[1024,1024]{1,0:T(8,128)(2,1)} %wv.3), custom_call_target="tpu_custom_call" | custom-call | flops 134217728 | bytes 4194304 | tf_op jit(solution)/shard_map/pallas_call | solution.py:326
  4.4 1.5 %collective-permute-start.1 = (bf16[256,256]{1,0:T(8,128)(2,1)S(1)}, bf16[256,256]{1,0:T(8,128)(2,1)S(1)}, u32[]{:S(2)}, u32[]{:S(2)}) collective-permute-start(bf16[256,256]{1,0:T(8,128)(2,1)S(1)} %get-tuple-element.39), channel_id=1, source_target_pairs={{0,2},{2,0},{4,6},{6,4},{1,3},{3,1},{5,7},{7,5},{8,10},{10,8},{12,... | collective-permute-start | bytes 393224 | tf_op jit(solution)/shard_map/ppermute | solution.py:320
  5.9 2.6 %collective-permute-start.2 = (bf16[256,256]{1,0:T(8,128)(2,1)S(1)}, bf16[256,256]{1,0:T(8,128)(2,1)S(1)}, u32[]{:S(2)}, u32[]{:S(2)}) collective-permute-start(bf16[256,256]{1,0:T(8,128)(2,1)S(1)} %get-tuple-element.40), channel_id=1, source_target_pairs={{0,4},{2,6},{4,0},{6,2},{1,5},{3,7},{5,1},{7,3},{8,12},{10,14},{12... | collective-permute-start | bytes 393224 | tf_op jit(solution)/shard_map/ppermute | solution.py:320
  8.6 1.9 %shard_map.115 = (bf16[256,128]{1,0:T(8,128)(2,1)S(1)}, bf16[256,128]{1,0:T(8,128)(2,1)S(1)}, bf16[256,128]{1,0:T(8,128)(2,1)S(1)}, bf16[256,128]{1,0:T(8,128)(2,1)S(1)}, bf16[256,256]{1,0:T(8,128)(2,1)S(1)}) custom-call(bf16[256,1024]{1,0:T(8,128)(2,1)S(1)} %get-tuple-element.33.normed, bf16[1024,1024]{1,0:T(8,128)(2,1)S(1)} %copy-done, ...), custom_call_target="tpu_custom_call" | custom-call | flops 268435456 | bytes 4194304 | tf_op jit(solution)/shard_map/pallas_call | solution.py:349
  10.5 4.4 %collective-permute-done.2.refs_2_ = bf16[256,256]{1,0:T(8,128)(2,1)S(1)} collective-permute-done((bf16[256,256]{1,0:T(8,128)(2,1)S(1)}, bf16[256,256]{1,0:T(8,128)(2,1)S(1)}, u32[]{:S(2)}, u32[]{:S(2)}) %collective-permute-start.2) | collective-permute-done | bytes 131104 | tf_op jit(solution)/shard_map/ppermute | solution.py:320
  14.9 2.5 %collective-permute-done.3.refs_3_ = bf16[256,256]{1,0:T(8,128)(2,1)S(1)} collective-permute-done((bf16[256,256]{1,0:T(8,128)(2,1)S(1)}, bf16[256,256]{1,0:T(8,128)(2,1)S(1)}, u32[]{:S(2)}, u32[]{:S(2)}) %collective-permute-start.3) | collective-permute-done | bytes 131104 | tf_op jit(solution)/shard_map/ppermute | solution.py:320
  17.5 1.7 %shard_map.116 = (bf16[520,128]{1,0:T(8,128)(2,1)S(1)}, bf16[520,128]{1,0:T(8,128)(2,1)S(1)}, f32[2,128,1024]{2,1,0:T(8,128)S(1)}, bf16[2048,128]{1,0:T(8,128)(2,1)S(1)}) custom-call(bf16[256,256]{1,0:T(8,128)(2,1)S(1)} %get-tuple-element.38.refs_0_, bf16[256,256]{1,0:T(8,128)(2,1)S(1)} %collective-permute-done.1.refs_1_, ...), custom_call_target="tpu_custom_call" | custom-call | flops 1090519040 | bytes 2097152 | tf_op jit(solution)/shard_map/pallas_call | solution.py:361
  20.0 3.8 %collective-permute-start.9 = (bf16[520,128]{1,0:T(8,128)(2,1)S(1)}, bf16[520,128]{1,0:T(8,128)(2,1)S(1)}, u32[]{:S(2)}, u32[]{:S(2)}) collective-permute-start(bf16[520,128]{1,0:T(8,128)(2,1)S(1)} %shard_map.117.after), channel_id=1, source_target_pairs={{0,24},{8,16},{16,8},{24,0},{1,25},{9,17},{17,9},{25,1},{2,26},{10... | collective-permute-start | bytes 399368 | tf_op jit(solution)/shard_map/ppermute | solution.py:376
  23.8 1.3 %collective-permute-start.8 = (bf16[520,128]{1,0:T(8,128)(2,1)S(1)}, bf16[520,128]{1,0:T(8,128)(2,1)S(1)}, u32[]{:S(2)}, u32[]{:S(2)}) collective-permute-start(bf16[520,128]{1,0:T(8,128)(2,1)S(1)} %get-tuple-element.49), channel_id=1, source_target_pairs={{0,16},{8,24},{16,0},{24,8},{1,17},{9,25},{17,1},{25,9},{2,18},{10... | collective-permute-start | bytes 399368 | tf_op jit(solution)/shard_map/ppermute | solution.py:376
  25.1 1.2 %collective-permute-start.5 = (bf16[256,128]{1,0:T(8,128)(2,1)S(1)}, bf16[256,128]{1,0:T(8,128)(2,1)S(1)}, u32[]{:S(2)}, u32[]{:S(2)}) collective-permute-start(bf16[256,128]{1,0:T(8,128)(2,1)S(1)} %get-tuple-element.46), channel_id=1, source_target_pairs={{0,4},{2,6},{4,0},{6,2},{1,5},{3,7},{5,1},{7,3},{8,12},{10,14},{12... | collective-permute-start | bytes 196616 | tf_op jit(solution)/shard_map/ppermute | solution.py:320
  26.9 2.1 %collective-permute-start.6 = (bf16[256,128]{1,0:T(8,128)(2,1)S(1)}, bf16[256,128]{1,0:T(8,128)(2,1)S(1)}, u32[]{:S(2)}, u32[]{:S(2)}) collective-permute-start(bf16[256,128]{1,0:T(8,128)(2,1)S(1)} %get-tuple-element.47), channel_id=1, source_target_pairs={{0,6},{2,4},{4,2},{6,0},{1,7},{3,5},{5,3},{7,1},{8,14},{10,12},{12... | collective-permute-start | bytes 196616 | tf_op jit(solution)/shard_map/ppermute | solution.py:320
  29.8 1.1 %collective-permute-done.8.refs_2_ = bf16[520,128]{1,0:T(8,128)(2,1)S(1)} collective-permute-done((bf16[520,128]{1,0:T(8,128)(2,1)S(1)}, bf16[520,128]{1,0:T(8,128)(2,1)S(1)}, u32[]{:S(2)}, u32[]{:S(2)}) %collective-permute-start.8) | collective-permute-done | bytes 133152 | tf_op jit(solution)/shard_map/ppermute | solution.py:376
  31.0 2.5 %collective-permute-start.12 = (bf16[520,128]{1,0:T(8,128)(2,1)S(1)}, bf16[520,128]{1,0:T(8,128)(2,1)S(1)}, u32[]{:S(2)}, u32[]{:S(2)}) collective-permute-start(bf16[520,128]{1,0:T(8,128)(2,1)S(1)} %shard_map.120.refs_4_), channel_id=1, source_target_pairs={{0,96},{32,64},{64,32},{96,0},{1,97},{33,65},{65,33},{97,1},{2,98}... | collective-permute-start | bytes 399368 | tf_op jit(solution)/shard_map/ppermute | solution.py:390
  34.3 2.2 %shard_map.118.refs_8_.refs_0_.phi = bf16[2080,2048]{1,0:T(8,128)(2,1)S(1)} custom-call(bf16[256,128]{1,0:T(8,128)(2,1)S(1)} %get-tuple-element.44.refs_0_.refs_4_, bf16[256,128]{1,0:T(8,128)(2,1)S(1)} %collective-permute-done.4.refs_1_.refs_5_, bf16[256,128]{1,0:T(8,128)(2,1)S(1)} %collective-permute-done.5.refs_2_.refs_6_, ...), custom_call_target="tpu_custom_call" | custom-call | flops 545259520 | bytes 9437184 | tf_op jit(solution)/shard_map/pallas_call | solution.py:392
  36.5 2.1 %shard_map.121.refs_9_.refs_5_.inside = f32[1024,128]{1,0:T(8,128)S(1)} custom-call(bf16[256,256]{1,0:T(8,128)(2,1)S(1)} %get-tuple-element.38.refs_0_, bf16[256,256]{1,0:T(8,128)(2,1)S(1)} %collective-permute-done.1.refs_1_, bf16[256,256]{1,0:T(8,128)(2,1)S(1)} %collective-permute-done.2.refs_2_, bf16[256,256]{1,0:T(8,128)(2,1)S(1)} %collective-permute-done.3.refs_3_, ...), custom_call_target="tpu_custom_call" | custom-call | flops 1073741824 | bytes 2097152 | tf_op jit(solution)/shard_map/pallas_call | solution.py:379
  39.6 3.0 %collective-permute-start.14 = (bf16[520,128]{1,0:T(8,128)(2,1)S(1)}, bf16[520,128]{1,0:T(8,128)(2,1)S(1)}, u32[]{:S(2)}, u32[]{:S(2)}) collective-permute-start(bf16[520,128]{1,0:T(8,128)(2,1)S(1)} %get-tuple-element.52), channel_id=1, source_target_pairs={{0,16},{8,24},{16,0},{24,8},{1,17},{9,25},{17,1},{25,9},{2,18},{10... | collective-permute-start | bytes 399368 | tf_op jit(solution)/shard_map/ppermute | solution.py:320
  43.4 2.9 %collective-permute-done.14.refs_3_ = bf16[520,128]{1,0:T(8,128)(2,1)S(1)} collective-permute-done((bf16[520,128]{1,0:T(8,128)(2,1)S(1)}, bf16[520,128]{1,0:T(8,128)(2,1)S(1)}, u32[]{:S(2)}, u32[]{:S(2)}) %collective-permute-start.14) | collective-permute-done | bytes 133152 | tf_op jit(solution)/shard_map/ppermute | solution.py:320
  46.3 1.4 %collective-permute-done.15.refs_4_ = bf16[520,128]{1,0:T(8,128)(2,1)S(1)} collective-permute-done((bf16[520,128]{1,0:T(8,128)(2,1)S(1)}, bf16[520,128]{1,0:T(8,128)(2,1)S(1)}, u32[]{:S(2)}, u32[]{:S(2)}) %collective-permute-start.15) | collective-permute-done | bytes 133152 | tf_op jit(solution)/shard_map/ppermute | solution.py:320
  47.8 1.7 %shard_map.123 = (bf16[256,128]{1,0:T(8,128)(2,1)S(1)}, bf16[256,128]{1,0:T(8,128)(2,1)S(1)}, bf16[256,128]{1,0:T(8,128)(2,1)S(1)}, bf16[128,2080]{1,0:T(8,128)(2,1)S(1)}) custom-call(bf16[2080,2048]{1,0:T(8,128)(2,1)S(1)} %shard_map.118.refs_8_.refs_0_.phi, bf16[520,128]{1,0:T(8,128)(2,1)S(1)} %get-tuple-element.50.refs_1_, ...), custom_call_target="tpu_custom_call" | custom-call | flops 1635778560 | bytes 2097152 | tf_op jit(solution)/shard_map/pallas_call | solution.py:407
  49.5 3.5 %collective-permute-start.16 = (bf16[256,128]{1,0:T(8,128)(2,1)S(1)}, bf16[256,128]{1,0:T(8,128)(2,1)S(1)}, u32[]{:S(2)}, u32[]{:S(2)}) collective-permute-start(bf16[256,128]{1,0:T(8,128)(2,1)S(1)} %get-tuple-element.55), channel_id=1, source_target_pairs={{0,3},{1,2},{2,1},{3,0},{4,7},{5,6},{6,5},{7,4},{8,11},{9,10},{10,... | collective-permute-start | bytes 196616 | tf_op jit(solution)/shard_map/ppermute | solution.py:417
  53.7 5.0 %collective-permute-start.18 = (bf16[256,128]{1,0:T(8,128)(2,1)S(1)}, bf16[256,128]{1,0:T(8,128)(2,1)S(1)}, u32[]{:S(2)}, u32[]{:S(2)}) collective-permute-start(bf16[256,128]{1,0:T(8,128)(2,1)S(1)} %get-tuple-element.57), channel_id=1, source_target_pairs={{0,7},{1,6},{2,5},{3,4},{4,3},{5,2},{6,1},{7,0},{8,15},{9,14},{10,... | collective-permute-start | bytes 196616 | tf_op jit(solution)/shard_map/ppermute | solution.py:417
  59.5 1.9 %collective-permute-done.18.refs_3_ = bf16[256,128]{1,0:T(8,128)(2,1)S(1)} collective-permute-done((bf16[256,128]{1,0:T(8,128)(2,1)S(1)}, bf16[256,128]{1,0:T(8,128)(2,1)S(1)}, u32[]{:S(2)}, u32[]{:S(2)}) %collective-permute-start.18) | collective-permute-done | bytes 65568 | tf_op jit(solution)/shard_map/ppermute | solution.py:417
  62.9 4.0 %shard_map.126 = (bf16[128,1024]{1,0:T(8,128)(2,1)}, bf16[128,1024]{1,0:T(8,128)(2,1)}) custom-call(bf16[256,128]{1,0:T(8,128)(2,1)S(1)} %shard_map.124.refs_0_, bf16[256,128]{1,0:T(8,128)(2,1)S(1)} %collective-permute-done.16.refs_1_, bf16[256,128]{1,0:T(8,128)(2,1)S(1)} %collective-permute-done.17.refs_2_, ...), custom_call_target="tpu_custom_call" | custom-call | flops 2415919104 | bytes 18874368 | tf_op jit(solution)/shard_map/pallas_call | solution.py:425
  (50 shorter events, 8.6 us)
Async XLA Ops:
  0.6 3.1 %collective-permute-start = (bf16[128,1024]{1,0:T(8,128)(2,1)}, bf16[128,1024]{1,0:T(8,128)(2,1)S(1)}, u32[]{:S(2)}, u32[]{:S(2)}) collective-permute-start(bf16[128,1024]{1,0:T(8,128)(2,1)} %refs_5_.1), channel_id=1, source_target_pairs={{0,1},{1,0},{2,3},{3,2},{4,5},{5,4},{6,7},{7,6},{8,9},{9,8},{10,11... | collective-permute-start | bytes 786440 | tf_op jit(solution)/shard_map/ppermute | solution.py:325
  4.4 6.0 %collective-permute-start.1 = (bf16[256,256]{1,0:T(8,128)(2,1)S(1)}, bf16[256,256]{1,0:T(8,128)(2,1)S(1)}, u32[]{:S(2)}, u32[]{:S(2)}) collective-permute-start(bf16[256,256]{1,0:T(8,128)(2,1)S(1)} %get-tuple-element.39), channel_id=1, source_target_pairs={{0,2},{2,0},{4,6},{6,4},{1,3},{3,1},{5,7},{7,5},{8,10},{10,8},{12,... | collective-permute-start | bytes 393224 | tf_op jit(solution)/shard_map/ppermute | solution.py:320
  5.9 9.0 %collective-permute-start.2 = (bf16[256,256]{1,0:T(8,128)(2,1)S(1)}, bf16[256,256]{1,0:T(8,128)(2,1)S(1)}, u32[]{:S(2)}, u32[]{:S(2)}) collective-permute-start(bf16[256,256]{1,0:T(8,128)(2,1)S(1)} %get-tuple-element.40), channel_id=1, source_target_pairs={{0,4},{2,6},{4,0},{6,2},{1,5},{3,7},{5,1},{7,3},{8,12},{10,14},{12... | collective-permute-start | bytes 393224 | tf_op jit(solution)/shard_map/ppermute | solution.py:320
  8.6 8.9 %collective-permute-start.3 = (bf16[256,256]{1,0:T(8,128)(2,1)S(1)}, bf16[256,256]{1,0:T(8,128)(2,1)S(1)}, u32[]{:S(2)}, u32[]{:S(2)}) collective-permute-start(bf16[256,256]{1,0:T(8,128)(2,1)S(1)} %get-tuple-element.41), channel_id=1, source_target_pairs={{0,6},{2,4},{4,2},{6,0},{1,7},{3,5},{5,3},{7,1},{8,14},{10,12},{12... | collective-permute-start | bytes 393224 | tf_op jit(solution)/shard_map/ppermute | solution.py:320
  20.0 6.9 %collective-permute-start.9 = (bf16[520,128]{1,0:T(8,128)(2,1)S(1)}, bf16[520,128]{1,0:T(8,128)(2,1)S(1)}, u32[]{:S(2)}, u32[]{:S(2)}) collective-permute-start(bf16[520,128]{1,0:T(8,128)(2,1)S(1)} %shard_map.117.after), channel_id=1, source_target_pairs={{0,24},{8,16},{16,8},{24,0},{1,25},{9,17},{17,9},{25,1},{2,26},{10... | collective-permute-start | bytes 399368 | tf_op jit(solution)/shard_map/ppermute | solution.py:376
  23.8 6.0 %collective-permute-start.7 = (bf16[520,128]{1,0:T(8,128)(2,1)S(1)}, bf16[520,128]{1,0:T(8,128)(2,1)S(1)}, u32[]{:S(2)}, u32[]{:S(2)}) collective-permute-start(bf16[520,128]{1,0:T(8,128)(2,1)S(1)} %get-tuple-element.48), channel_id=1, source_target_pairs={{0,8},{8,0},{16,24},{24,16},{1,9},{9,1},{17,25},{25,17},{2,10},{10... | collective-permute-start | bytes 399368 | tf_op jit(solution)/shard_map/ppermute | solution.py:376
  23.8 7.1 %collective-permute-start.8 = (bf16[520,128]{1,0:T(8,128)(2,1)S(1)}, bf16[520,128]{1,0:T(8,128)(2,1)S(1)}, u32[]{:S(2)}, u32[]{:S(2)}) collective-permute-start(bf16[520,128]{1,0:T(8,128)(2,1)S(1)} %get-tuple-element.49), channel_id=1, source_target_pairs={{0,16},{8,24},{16,0},{24,8},{1,17},{9,25},{17,1},{25,9},{2,18},{10... | collective-permute-start | bytes 399368 | tf_op jit(solution)/shard_map/ppermute | solution.py:376
  25.1 9.0 %collective-permute-start.4 = (bf16[256,128]{1,0:T(8,128)(2,1)S(1)}, bf16[256,128]{1,0:T(8,128)(2,1)S(1)}, u32[]{:S(2)}, u32[]{:S(2)}) collective-permute-start(bf16[256,128]{1,0:T(8,128)(2,1)S(1)} %get-tuple-element.45), channel_id=1, source_target_pairs={{0,2},{2,0},{4,6},{6,4},{1,3},{3,1},{5,7},{7,5},{8,10},{10,8},{12,... | collective-permute-start | bytes 196616 | tf_op jit(solution)/shard_map/ppermute | solution.py:320
  25.1 9.2 %collective-permute-start.5 = (bf16[256,128]{1,0:T(8,128)(2,1)S(1)}, bf16[256,128]{1,0:T(8,128)(2,1)S(1)}, u32[]{:S(2)}, u32[]{:S(2)}) collective-permute-start(bf16[256,128]{1,0:T(8,128)(2,1)S(1)} %get-tuple-element.46), channel_id=1, source_target_pairs={{0,4},{2,6},{4,0},{6,2},{1,5},{3,7},{5,1},{7,3},{8,12},{10,14},{12... | collective-permute-start | bytes 196616 | tf_op jit(solution)/shard_map/ppermute | solution.py:320
  26.9 7.4 %collective-permute-start.6 = (bf16[256,128]{1,0:T(8,128)(2,1)S(1)}, bf16[256,128]{1,0:T(8,128)(2,1)S(1)}, u32[]{:S(2)}, u32[]{:S(2)}) collective-permute-start(bf16[256,128]{1,0:T(8,128)(2,1)S(1)} %get-tuple-element.47), channel_id=1, source_target_pairs={{0,6},{2,4},{4,2},{6,0},{1,7},{3,5},{5,3},{7,1},{8,14},{10,12},{12... | collective-permute-start | bytes 196616 | tf_op jit(solution)/shard_map/ppermute | solution.py:320
  31.0 7.6 %collective-permute-start.12 = (bf16[520,128]{1,0:T(8,128)(2,1)S(1)}, bf16[520,128]{1,0:T(8,128)(2,1)S(1)}, u32[]{:S(2)}, u32[]{:S(2)}) collective-permute-start(bf16[520,128]{1,0:T(8,128)(2,1)S(1)} %shard_map.120.refs_4_), channel_id=1, source_target_pairs={{0,96},{32,64},{64,32},{96,0},{1,97},{33,65},{65,33},{97,1},{2,98}... | collective-permute-start | bytes 399368 | tf_op jit(solution)/shard_map/ppermute | solution.py:390
  33.5 5.4 %collective-permute-start.11 = (bf16[520,128]{1,0:T(8,128)(2,1)S(1)}, bf16[520,128]{1,0:T(8,128)(2,1)S(1)}, u32[]{:S(2)}, u32[]{:S(2)}) collective-permute-start(bf16[520,128]{1,0:T(8,128)(2,1)S(1)} %shard_map.120.refs_4_), channel_id=1, source_target_pairs={{0,64},{32,96},{64,0},{96,32},{1,65},{33,97},{65,1},{97,33},{2,66}... | collective-permute-start | bytes 399368 | tf_op jit(solution)/shard_map/ppermute | solution.py:390
  34.0 5.0 %collective-permute-start.10 = (bf16[520,128]{1,0:T(8,128)(2,1)S(1)}, bf16[520,128]{1,0:T(8,128)(2,1)S(1)}, u32[]{:S(2)}, u32[]{:S(2)}) collective-permute-start(bf16[520,128]{1,0:T(8,128)(2,1)S(1)} %shard_map.120.refs_4_), channel_id=1, source_target_pairs={{0,32},{32,0},{64,96},{96,64},{1,33},{33,1},{65,97},{97,65},{2,34}... | collective-permute-start | bytes 399368 | tf_op jit(solution)/shard_map/ppermute | solution.py:390
  38.6 9.2 %copy-start.4 = (f32[128]{0:T(128)S(1)}, f32[128]{0:T(128)}, u32[]{:S(2)}) copy-start(f32[128]{0:T(128)} %param.15) | copy-start | bytes 1540
  39.0 23.8 %slice-start.2 = ((s8[8388608]{0:T(1024)(128)(4,1)}), s8[4194304]{0:T(1024)(128)(4,1)S(1)}, s32[]{:S(2)}) async-start(s8[8388608]{0:T(1024)(128)(4,1)} %bitcast.5), calls=%async_computation.2 | async-start | bytes 8388608
  39.5 3.9 %collective-permute-start.13 = (bf16[520,128]{1,0:T(8,128)(2,1)S(1)}, bf16[520,128]{1,0:T(8,128)(2,1)S(1)}, u32[]{:S(2)}, u32[]{:S(2)}) collective-permute-start(bf16[520,128]{1,0:T(8,128)(2,1)S(1)} %get-tuple-element.51), channel_id=1, source_target_pairs={{0,8},{8,0},{16,24},{24,16},{1,9},{9,1},{17,25},{25,17},{2,10},{10... | collective-permute-start | bytes 399368 | tf_op jit(solution)/shard_map/ppermute | solution.py:320
  39.6 6.8 %collective-permute-start.14 = (bf16[520,128]{1,0:T(8,128)(2,1)S(1)}, bf16[520,128]{1,0:T(8,128)(2,1)S(1)}, u32[]{:S(2)}, u32[]{:S(2)}) collective-permute-start(bf16[520,128]{1,0:T(8,128)(2,1)S(1)} %get-tuple-element.52), channel_id=1, source_target_pairs={{0,16},{8,24},{16,0},{24,8},{1,17},{9,25},{17,1},{25,9},{2,18},{10... | collective-permute-start | bytes 399368 | tf_op jit(solution)/shard_map/ppermute | solution.py:320
  42.5 5.2 %collective-permute-start.15 = (bf16[520,128]{1,0:T(8,128)(2,1)S(1)}, bf16[520,128]{1,0:T(8,128)(2,1)S(1)}, u32[]{:S(2)}, u32[]{:S(2)}) collective-permute-start(bf16[520,128]{1,0:T(8,128)(2,1)S(1)} %get-tuple-element.53), channel_id=1, source_target_pairs={{0,24},{8,16},{16,8},{24,0},{1,25},{9,17},{17,9},{25,1},{2,26},{10... | collective-permute-start | bytes 399368 | tf_op jit(solution)/shard_map/ppermute | solution.py:320
  47.7 15.1 %slice-start = ((s8[8388608]{0:T(1024)(128)(4,1)}), s8[4194304]{0:T(1024)(128)(4,1)S(1)}, s32[]{:S(2)}) async-start(s8[8388608]{0:T(1024)(128)(4,1)} %bitcast.3), calls=%async_computation | async-start | bytes 8388608
  47.8 15.1 %slice-start.3 = ((s8[8388608]{0:T(1024)(128)(4,1)}), s8[4194304]{0:T(1024)(128)(4,1)S(1)}, s32[]{:S(2)}) async-start(s8[8388608]{0:T(1024)(128)(4,1)} %bitcast.5), calls=%async_computation.3 | async-start | bytes 8388608
  49.5 10.0 %collective-permute-start.16 = (bf16[256,128]{1,0:T(8,128)(2,1)S(1)}, bf16[256,128]{1,0:T(8,128)(2,1)S(1)}, u32[]{:S(2)}, u32[]{:S(2)}) collective-permute-start(bf16[256,128]{1,0:T(8,128)(2,1)S(1)} %get-tuple-element.55), channel_id=1, source_target_pairs={{0,3},{1,2},{2,1},{3,0},{4,7},{5,6},{6,5},{7,4},{8,11},{9,10},{10,... | collective-permute-start | bytes 196616 | tf_op jit(solution)/shard_map/ppermute | solution.py:417
  53.0 6.5 %collective-permute-start.17 = (bf16[256,128]{1,0:T(8,128)(2,1)S(1)}, bf16[256,128]{1,0:T(8,128)(2,1)S(1)}, u32[]{:S(2)}, u32[]{:S(2)}) collective-permute-start(bf16[256,128]{1,0:T(8,128)(2,1)S(1)} %get-tuple-element.56), channel_id=1, source_target_pairs={{0,5},{1,4},{2,7},{3,6},{4,1},{5,0},{6,3},{7,2},{8,13},{9,12},{10,... | collective-permute-start | bytes 196616 | tf_op jit(solution)/shard_map/ppermute | solution.py:417
  53.7 7.7 %collective-permute-start.18 = (bf16[256,128]{1,0:T(8,128)(2,1)S(1)}, bf16[256,128]{1,0:T(8,128)(2,1)S(1)}, u32[]{:S(2)}, u32[]{:S(2)}) collective-permute-start(bf16[256,128]{1,0:T(8,128)(2,1)S(1)} %get-tuple-element.57), channel_id=1, source_target_pairs={{0,7},{1,6},{2,5},{3,4},{4,3},{5,2},{6,1},{7,0},{8,15},{9,14},{10,... | collective-permute-start | bytes 196616 | tf_op jit(solution)/shard_map/ppermute | solution.py:417
  61.4 1.5 %collective-permute-start.19 = (bf16[128,512]{1,0:T(8,128)(2,1)S(1)}, bf16[128,512]{1,0:T(8,128)(2,1)S(1)}, u32[]{:S(2)}, u32[]{:S(2)}) collective-permute-start(bf16[128,512]{1,0:T(8,128)(2,1)S(1)} %shard_map.125), channel_id=1, source_target_pairs={{0,1},{1,0},{2,3},{3,2},{4,5},{5,4},{6,7},{7,6},{8,9},{9,8},{10,11... | collective-permute-start | bytes 393224 | tf_op jit(solution)/shard_map/ppermute | solution.py:423
  (5 other events, 21.5 us)

commit v2 on v1

--- a/solution.py
+++ b/solution.py
@@ -313,12 +313,15 @@
     return pltpu.with_memory_space_constraint(array, pltpu.HBM)
 
 
-ORDER = (2, 3, 1)
-
-
-def exchange(parts, axis):
-    moved = {k: lax.ppermute(parts[k], axis, xor_pairs(4, k)) for k in ORDER}
-    return [parts[0]] + [moved[k] for k in range(1, 4)]
+def exchange(parts, axes, pairs):
+    moved = [parts[0]]
+    for k in range(1, 4):
+        moved.append(lax.ppermute(parts[k], axes, pairs[k]))
+    return moved
+
+
+ALONG = {k: xor_pairs(4, k) for k in range(1, 4)}
+SWAPS = {k: [(i, i ^ (2 * k + 1)) for i in range(8)] for k in range(1, 4)}
 
 
 def body(tokens, attn_gain, w_query, w_key, w_value, head_gain, w_output, mlp_gain, w_in, w_out):
@@ -345,7 +348,7 @@
         flops=2 * 256 * 1024 * 1024,
         moved=3 * MIB,
     )(own, swapped, gain, wkv)
-    pairs = exchange([None, *pairs], "y")
+    pairs = exchange([None, *pairs], "y", ALONG)
     *queries, pairs[0] = call(
         q_kernel,
         [arr(PAIR, 128)] * 4 + [arr(PAIR, 256)],
@@ -371,11 +374,9 @@
     own = call(
         rest_kernel, arr(PIECE, 128), spare, [VM] * 2 + [ANY], 8, flops=cost, moved=MIB
     )(ext, vz, third)
-    pieces = [own]
-    for k, piece in ((1, first), (2, second), (3, third)):
-        pieces.append(lax.ppermute(piece, "z", xor_pairs(4, k)))
+    pieces = exchange([own, first, second, third], "z", ALONG)
     queries = lax.optimization_barrier((queries, third))[0]
-    queries = exchange(queries, "y")
+    queries = exchange(queries, "y", ALONG)
     inside = call(
         inside_kernel,
         arr(LEN, 128, dtype=F32),
@@ -387,8 +388,7 @@
     )(*pairs, *queries)
 
     total = call(total_kernel, arr(PIECE, 128), [], [VM] * 4, 4, moved=MIB)(*pieces)
-    moved = {k: lax.ppermute(total, "x", xor_pairs(4, k)) for k in ORDER}
-    totals = [total] + [moved[k] for k in range(1, 4)]
+    totals = exchange([total] * 4, "x", ALONG)
     phi = call(
         features_kernel,
         arr(NF, 2 * LEN),
@@ -401,7 +401,7 @@
     states = call(
         combine_kernel, [arr(PIECE, 128)] * 4, [], [VM] * 8 + [ANY] * 2, 8, moved=MIB
     )(*pieces, *totals, phi, inside)
-    states = exchange(states, "z")
+    states = exchange(states, "z", ALONG)
 
     scale = head_gain.reshape(1, 128)
     *parts, turned = call(
@@ -413,12 +413,11 @@
         flops=2 * NF * 2 * LEN * 192,
         moved=2 * MIB,
     )(phi, *states, inside, scale)
-    swaps = {k: [(i, i ^ (2 * k + 1)) for i in range(8)] for k in ORDER}
-    moved = {k: lax.ppermute(parts[k - 1], ("y", "c"), swaps[k]) for k in ORDER}
+    home = exchange([None, *parts], ("y", "c"), SWAPS)
     mine = call(
         own_kernel, arr(PAIR, 128), [], [VM] * 4, 8, flops=2 * NF * 2 * LEN * 64, moved=2 * MIB
     )(phi, turned, inside, scale)
-    parts = [mine] + [moved[k] for k in range(1, 4)]
+    parts = [mine, *home[1:]]
     other = call(merge_kernel, arr(ROWS, 512), [], [VM] * 4, 4)(*parts)
     other = lax.ppermute(other, "c", xor_pairs(2, 1))
 

time: 67 us -> 67 us (level)
  no operation moved by 1% of the time
where the time goes in v2:
time: 67 us; the launch traced here: 66.9 us
  starting transfers between devices  30.9 us (46%)
  Pallas kernels  18.7 us (28%)
  waiting for transfers between devices  16.3 us (24%)
  between operations  0.84 us (1%)
    ppermute x18, starting transfers between devices, exchange(): moved.append(lax.ppermute(parts[k], axes, pairs[k]))  29 us
    ppermute x18, waiting for transfers between devices, exchange(): moved.append(lax.ppermute(parts[k], axes, pairs[k]))  15.3 us
    pallas_call x1, Pallas kernels, body(): call(mlp_kernel, [arr(ROWS, D)] * 2, [], [VM] * 10, 8, flops=2 * 128 * 10...  3.96 us
    pallas_call x1, Pallas kernels, body(): call(features_kernel, arr(NF, 2 * LEN), [pltpu.VMEM((2, 2 * HS, LEN), F32...  2.16 us
    pallas_call x1, Pallas kernels, body(): call(inside_kernel, arr(LEN, 128, dtype=F32), [pltpu.VMEM((LEN, 128), BF)...  2.08 us
    pallas_call x1, Pallas kernels, body(): call(q_kernel, [arr(PAIR, 128)] * 4 + [arr(PAIR, 256)], [pltpu.VMEM((D, 2...  1.91 us
    pallas_call x1, Pallas kernels, body(): call(apply_kernel, [arr(PAIR, 128)] * 3 + [arr(128, NF)], [pltpu.VMEM((NF...  1.72 us
    pallas_call x1, Pallas kernels, body(): call(state_kernel, [arr(PIECE, 128)] * 2 + [arr(2, 2 * HS, LEN, dtype=F32...  1.69 us
  transfers between devices with their start and end apart: 20, of which 10 were waited for; matrix products, arithmetic and copies ran while one was open for 0% of the time, Pallas kernels for 14%

profile of v2, /device:TPU:1, one launch (start us, length us, event | category | flops | bytes accessed | tf_op | source)
XLA Modules:
  0.0 66.9 jit_solution(17880522860439096970)
XLA Ops:
  0.6 1.5 %collective-permute-start = (bf16[128,1024]{1,0:T(8,128)(2,1)}, bf16[128,1024]{1,0:T(8,128)(2,1)S(1)}, u32[]{:S(2)}, u32[]{:S(2)}) collective-permute-start(bf16[128,1024]{1,0:T(8,128)(2,1)} %refs_5_.1), channel_id=1, source_target_pairs={{0,1},{1,0},{2,3},{3,2},{4,5},{5,4},{6,7},{7,6},{8,9},{9,8},{10,11... | collective-permute-start | bytes 786440 | tf_op jit(solution)/shard_map/ppermute | solution.py:328
  2.1 1.6 %shard_map.113 = (bf16[128,1024]{1,0:T(8,128)(2,1)S(1)}, f32[1,1024]{1,0:T(1,128)S(1)}, bf16[3,1024,256]{2,1,0:T(8,128)(2,1)S(1)}) custom-call(bf16[128,1024]{1,0:T(8,128)(2,1)} %refs_5_.1, f32[1,1024]{1,0:T(1,128)} %bitcast.10, bf16[1024,1024]{1,0:T(8,128)(2,1)} %wk.3, bf16[1024,1024]{1,0:T(8,128)(2,1)} %wv.3), custom_call_target="tpu_custom_call" | custom-call | flops 134217728 | bytes 4194304 | tf_op jit(solution)/shard_map/pallas_call | solution.py:329
  4.4 1.5 %collective-permute-start.1 = (bf16[256,256]{1,0:T(8,128)(2,1)S(1)}, bf16[256,256]{1,0:T(8,128)(2,1)S(1)}, u32[]{:S(2)}, u32[]{:S(2)}) collective-permute-start(bf16[256,256]{1,0:T(8,128)(2,1)S(1)} %get-tuple-element.39), channel_id=1, source_target_pairs={{0,2},{2,0},{4,6},{6,4},{1,3},{3,1},{5,7},{7,5},{8,10},{10,8},{12,... | collective-permute-start | bytes 393224 | tf_op jit(solution)/shard_map/ppermute | solution.py:319
  5.9 2.6 %collective-permute-start.2 = (bf16[256,256]{1,0:T(8,128)(2,1)S(1)}, bf16[256,256]{1,0:T(8,128)(2,1)S(1)}, u32[]{:S(2)}, u32[]{:S(2)}) collective-permute-start(bf16[256,256]{1,0:T(8,128)(2,1)S(1)} %get-tuple-element.40), channel_id=1, source_target_pairs={{0,4},{2,6},{4,0},{6,2},{1,5},{3,7},{5,1},{7,3},{8,12},{10,14},{12... | collective-permute-start | bytes 393224 | tf_op jit(solution)/shard_map/ppermute | solution.py:319
  8.6 1.9 %shard_map.115 = (bf16[256,128]{1,0:T(8,128)(2,1)S(1)}, bf16[256,128]{1,0:T(8,128)(2,1)S(1)}, bf16[256,128]{1,0:T(8,128)(2,1)S(1)}, bf16[256,128]{1,0:T(8,128)(2,1)S(1)}, bf16[256,256]{1,0:T(8,128)(2,1)S(1)}) custom-call(bf16[256,1024]{1,0:T(8,128)(2,1)S(1)} %get-tuple-element.33.normed, bf16[1024,1024]{1,0:T(8,128)(2,1)S(1)} %copy-done, ...), custom_call_target="tpu_custom_call" | custom-call | flops 268435456 | bytes 4194304 | tf_op jit(solution)/shard_map/pallas_call | solution.py:352
  10.5 4.4 %collective-permute-done.2.refs_2_ = bf16[256,256]{1,0:T(8,128)(2,1)S(1)} collective-permute-done((bf16[256,256]{1,0:T(8,128)(2,1)S(1)}, bf16[256,256]{1,0:T(8,128)(2,1)S(1)}, u32[]{:S(2)}, u32[]{:S(2)}) %collective-permute-start.2) | collective-permute-done | bytes 131104 | tf_op jit(solution)/shard_map/ppermute | solution.py:319
  14.9 2.5 %collective-permute-done.3.refs_3_ = bf16[256,256]{1,0:T(8,128)(2,1)S(1)} collective-permute-done((bf16[256,256]{1,0:T(8,128)(2,1)S(1)}, bf16[256,256]{1,0:T(8,128)(2,1)S(1)}, u32[]{:S(2)}, u32[]{:S(2)}) %collective-permute-start.3) | collective-permute-done | bytes 131104 | tf_op jit(solution)/shard_map/ppermute | solution.py:319
  17.5 1.7 %shard_map.116 = (bf16[520,128]{1,0:T(8,128)(2,1)S(1)}, bf16[520,128]{1,0:T(8,128)(2,1)S(1)}, f32[2,128,1024]{2,1,0:T(8,128)S(1)}, bf16[2048,128]{1,0:T(8,128)(2,1)S(1)}) custom-call(bf16[256,256]{1,0:T(8,128)(2,1)S(1)} %get-tuple-element.38.refs_0_, bf16[256,256]{1,0:T(8,128)(2,1)S(1)} %collective-permute-done.1.refs_1_, ...), custom_call_target="tpu_custom_call" | custom-call | flops 1090519040 | bytes 2097152 | tf_op jit(solution)/shard_map/pallas_call | solution.py:364
  20.0 3.8 %collective-permute-start.9 = (bf16[520,128]{1,0:T(8,128)(2,1)S(1)}, bf16[520,128]{1,0:T(8,128)(2,1)S(1)}, u32[]{:S(2)}, u32[]{:S(2)}) collective-permute-start(bf16[520,128]{1,0:T(8,128)(2,1)S(1)} %shard_map.117.after), channel_id=1, source_target_pairs={{0,24},{8,16},{16,8},{24,0},{1,25},{9,17},{17,9},{25,1},{2,26},{10... | collective-permute-start | bytes 399368 | tf_op jit(solution)/shard_map/ppermute | solution.py:319
  23.8 1.3 %collective-permute-start.8 = (bf16[520,128]{1,0:T(8,128)(2,1)S(1)}, bf16[520,128]{1,0:T(8,128)(2,1)S(1)}, u32[]{:S(2)}, u32[]{:S(2)}) collective-permute-start(bf16[520,128]{1,0:T(8,128)(2,1)S(1)} %get-tuple-element.49), channel_id=1, source_target_pairs={{0,16},{8,24},{16,0},{24,8},{1,17},{9,25},{17,1},{25,9},{2,18},{10... | collective-permute-start | bytes 399368 | tf_op jit(solution)/shard_map/ppermute | solution.py:319
  25.1 1.2 %collective-permute-start.5 = (bf16[256,128]{1,0:T(8,128)(2,1)S(1)}, bf16[256,128]{1,0:T(8,128)(2,1)S(1)}, u32[]{:S(2)}, u32[]{:S(2)}) collective-permute-start(bf16[256,128]{1,0:T(8,128)(2,1)S(1)} %get-tuple-element.46), channel_id=1, source_target_pairs={{0,4},{2,6},{4,0},{6,2},{1,5},{3,7},{5,1},{7,3},{8,12},{10,14},{12... | collective-permute-start | bytes 196616 | tf_op jit(solution)/shard_map/ppermute | solution.py:319
  26.9 2.1 %collective-permute-start.6 = (bf16[256,128]{1,0:T(8,128)(2,1)S(1)}, bf16[256,128]{1,0:T(8,128)(2,1)S(1)}, u32[]{:S(2)}, u32[]{:S(2)}) collective-permute-start(bf16[256,128]{1,0:T(8,128)(2,1)S(1)} %get-tuple-element.47), channel_id=1, source_target_pairs={{0,6},{2,4},{4,2},{6,0},{1,7},{3,5},{5,3},{7,1},{8,14},{10,12},{12... | collective-permute-start | bytes 196616 | tf_op jit(solution)/shard_map/ppermute | solution.py:319
  29.8 1.1 %collective-permute-done.8.refs_2_ = bf16[520,128]{1,0:T(8,128)(2,1)S(1)} collective-permute-done((bf16[520,128]{1,0:T(8,128)(2,1)S(1)}, bf16[520,128]{1,0:T(8,128)(2,1)S(1)}, u32[]{:S(2)}, u32[]{:S(2)}) %collective-permute-start.8) | collective-permute-done | bytes 133152 | tf_op jit(solution)/shard_map/ppermute | solution.py:319
  31.0 2.5 %collective-permute-start.12 = (bf16[520,128]{1,0:T(8,128)(2,1)S(1)}, bf16[520,128]{1,0:T(8,128)(2,1)S(1)}, u32[]{:S(2)}, u32[]{:S(2)}) collective-permute-start(bf16[520,128]{1,0:T(8,128)(2,1)S(1)} %shard_map.120.refs_4_), channel_id=1, source_target_pairs={{0,96},{32,64},{64,32},{96,0},{1,97},{33,65},{65,33},{97,1},{2,98}... | collective-permute-start | bytes 399368 | tf_op jit(solution)/shard_map/ppermute | solution.py:319
  34.3 2.2 %shard_map.118.refs_8_.refs_0_.phi = bf16[2080,2048]{1,0:T(8,128)(2,1)S(1)} custom-call(bf16[256,128]{1,0:T(8,128)(2,1)S(1)} %get-tuple-element.44.refs_0_.refs_4_, bf16[256,128]{1,0:T(8,128)(2,1)S(1)} %collective-permute-done.4.refs_1_.refs_5_, bf16[256,128]{1,0:T(8,128)(2,1)S(1)} %collective-permute-done.5.refs_2_.refs_6_, ...), custom_call_target="tpu_custom_call" | custom-call | flops 545259520 | bytes 9437184 | tf_op jit(solution)/shard_map/pallas_call | solution.py:392
  36.5 2.1 %shard_map.121.refs_9_.refs_5_.inside = f32[1024,128]{1,0:T(8,128)S(1)} custom-call(bf16[256,256]{1,0:T(8,128)(2,1)S(1)} %get-tuple-element.38.refs_0_, bf16[256,256]{1,0:T(8,128)(2,1)S(1)} %collective-permute-done.1.refs_1_, bf16[256,256]{1,0:T(8,128)(2,1)S(1)} %collective-permute-done.2.refs_2_, bf16[256,256]{1,0:T(8,128)(2,1)S(1)} %collective-permute-done.3.refs_3_, ...), custom_call_target="tpu_custom_call" | custom-call | flops 1073741824 | bytes 2097152 | tf_op jit(solution)/shard_map/pallas_call | solution.py:380
  39.6 3.0 %collective-permute-start.14 = (bf16[520,128]{1,0:T(8,128)(2,1)S(1)}, bf16[520,128]{1,0:T(8,128)(2,1)S(1)}, u32[]{:S(2)}, u32[]{:S(2)}) collective-permute-start(bf16[520,128]{1,0:T(8,128)(2,1)S(1)} %get-tuple-element.52), channel_id=1, source_target_pairs={{0,16},{8,24},{16,0},{24,8},{1,17},{9,25},{17,1},{25,9},{2,18},{10... | collective-permute-start | bytes 399368 | tf_op jit(solution)/shard_map/ppermute | solution.py:319
  43.4 2.9 %collective-permute-done.14.refs_3_ = bf16[520,128]{1,0:T(8,128)(2,1)S(1)} collective-permute-done((bf16[520,128]{1,0:T(8,128)(2,1)S(1)}, bf16[520,128]{1,0:T(8,128)(2,1)S(1)}, u32[]{:S(2)}, u32[]{:S(2)}) %collective-permute-start.14) | collective-permute-done | bytes 133152 | tf_op jit(solution)/shard_map/ppermute | solution.py:319
  46.3 1.4 %collective-permute-done.15.refs_4_ = bf16[520,128]{1,0:T(8,128)(2,1)S(1)} collective-permute-done((bf16[520,128]{1,0:T(8,128)(2,1)S(1)}, bf16[520,128]{1,0:T(8,128)(2,1)S(1)}, u32[]{:S(2)}, u32[]{:S(2)}) %collective-permute-start.15) | collective-permute-done | bytes 133152 | tf_op jit(solution)/shard_map/ppermute | solution.py:319
  47.8 1.7 %shard_map.123 = (bf16[256,128]{1,0:T(8,128)(2,1)S(1)}, bf16[256,128]{1,0:T(8,128)(2,1)S(1)}, bf16[256,128]{1,0:T(8,128)(2,1)S(1)}, bf16[128,2080]{1,0:T(8,128)(2,1)S(1)}) custom-call(bf16[2080,2048]{1,0:T(8,128)(2,1)S(1)} %shard_map.118.refs_8_.refs_0_.phi, bf16[520,128]{1,0:T(8,128)(2,1)S(1)} %get-tuple-element.50.refs_1_, ...), custom_call_target="tpu_custom_call" | custom-call | flops 1635778560 | bytes 2097152 | tf_op jit(solution)/shard_map/pallas_call | solution.py:407
  49.5 3.5 %collective-permute-start.16 = (bf16[256,128]{1,0:T(8,128)(2,1)S(1)}, bf16[256,128]{1,0:T(8,128)(2,1)S(1)}, u32[]{:S(2)}, u32[]{:S(2)}) collective-permute-start(bf16[256,128]{1,0:T(8,128)(2,1)S(1)} %get-tuple-element.55), channel_id=1, source_target_pairs={{0,3},{1,2},{2,1},{3,0},{4,7},{5,6},{6,5},{7,4},{8,11},{9,10},{10,... | collective-permute-start | bytes 196616 | tf_op jit(solution)/shard_map/ppermute | solution.py:319
  53.7 5.0 %collective-permute-start.18 = (bf16[256,128]{1,0:T(8,128)(2,1)S(1)}, bf16[256,128]{1,0:T(8,128)(2,1)S(1)}, u32[]{:S(2)}, u32[]{:S(2)}) collective-permute-start(bf16[256,128]{1,0:T(8,128)(2,1)S(1)} %get-tuple-element.57), channel_id=1, source_target_pairs={{0,7},{1,6},{2,5},{3,4},{4,3},{5,2},{6,1},{7,0},{8,15},{9,14},{10,... | collective-permute-start | bytes 196616 | tf_op jit(solution)/shard_map/ppermute | solution.py:319
  59.5 1.9 %collective-permute-done.18.refs_3_ = bf16[256,128]{1,0:T(8,128)(2,1)S(1)} collective-permute-done((bf16[256,128]{1,0:T(8,128)(2,1)S(1)}, bf16[256,128]{1,0:T(8,128)(2,1)S(1)}, u32[]{:S(2)}, u32[]{:S(2)}) %collective-permute-start.18) | collective-permute-done | bytes 65568 | tf_op jit(solution)/shard_map/ppermute | solution.py:319
  62.9 4.0 %shard_map.126 = (bf16[128,1024]{1,0:T(8,128)(2,1)}, bf16[128,1024]{1,0:T(8,128)(2,1)}) custom-call(bf16[256,128]{1,0:T(8,128)(2,1)S(1)} %shard_map.124.refs_0_, bf16[256,128]{1,0:T(8,128)(2,1)S(1)} %collective-permute-done.16.refs_1_, bf16[256,128]{1,0:T(8,128)(2,1)S(1)} %collective-permute-done.17.refs_2_, ...), custom_call_target="tpu_custom_call" | custom-call | flops 2415919104 | bytes 18874368 | tf_op jit(solution)/shard_map/pallas_call | solution.py:424
  (50 shorter events, 8.6 us)
Async XLA Ops:
  0.6 3.1 %collective-permute-start = (bf16[128,1024]{1,0:T(8,128)(2,1)}, bf16[128,1024]{1,0:T(8,128)(2,1)S(1)}, u32[]{:S(2)}, u32[]{:S(2)}) collective-permute-start(bf16[128,1024]{1,0:T(8,128)(2,1)} %refs_5_.1), channel_id=1, source_target_pairs={{0,1},{1,0},{2,3},{3,2},{4,5},{5,4},{6,7},{7,6},{8,9},{9,8},{10,11... | collective-permute-start | bytes 786440 | tf_op jit(solution)/shard_map/ppermute | solution.py:328
  4.4 6.0 %collective-permute-start.1 = (bf16[256,256]{1,0:T(8,128)(2,1)S(1)}, bf16[256,256]{1,0:T(8,128)(2,1)S(1)}, u32[]{:S(2)}, u32[]{:S(2)}) collective-permute-start(bf16[256,256]{1,0:T(8,128)(2,1)S(1)} %get-tuple-element.39), channel_id=1, source_target_pairs={{0,2},{2,0},{4,6},{6,4},{1,3},{3,1},{5,7},{7,5},{8,10},{10,8},{12,... | collective-permute-start | bytes 393224 | tf_op jit(solution)/shard_map/ppermute | solution.py:319
  5.9 9.0 %collective-permute-start.2 = (bf16[256,256]{1,0:T(8,128)(2,1)S(1)}, bf16[256,256]{1,0:T(8,128)(2,1)S(1)}, u32[]{:S(2)}, u32[]{:S(2)}) collective-permute-start(bf16[256,256]{1,0:T(8,128)(2,1)S(1)} %get-tuple-element.40), channel_id=1, source_target_pairs={{0,4},{2,6},{4,0},{6,2},{1,5},{3,7},{5,1},{7,3},{8,12},{10,14},{12... | collective-permute-start | bytes 393224 | tf_op jit(solution)/shard_map/ppermute | solution.py:319
  8.6 8.9 %collective-permute-start.3 = (bf16[256,256]{1,0:T(8,128)(2,1)S(1)}, bf16[256,256]{1,0:T(8,128)(2,1)S(1)}, u32[]{:S(2)}, u32[]{:S(2)}) collective-permute-start(bf16[256,256]{1,0:T(8,128)(2,1)S(1)} %get-tuple-element.41), channel_id=1, source_target_pairs={{0,6},{2,4},{4,2},{6,0},{1,7},{3,5},{5,3},{7,1},{8,14},{10,12},{12... | collective-permute-start | bytes 393224 | tf_op jit(solution)/shard_map/ppermute | solution.py:319
  20.0 6.9 %collective-permute-start.9 = (bf16[520,128]{1,0:T(8,128)(2,1)S(1)}, bf16[520,128]{1,0:T(8,128)(2,1)S(1)}, u32[]{:S(2)}, u32[]{:S(2)}) collective-permute-start(bf16[520,128]{1,0:T(8,128)(2,1)S(1)} %shard_map.117.after), channel_id=1, source_target_pairs={{0,24},{8,16},{16,8},{24,0},{1,25},{9,17},{17,9},{25,1},{2,26},{10... | collective-permute-start | bytes 399368 | tf_op jit(solution)/shard_map/ppermute | solution.py:319
  23.8 6.0 %collective-permute-start.7 = (bf16[520,128]{1,0:T(8,128)(2,1)S(1)}, bf16[520,128]{1,0:T(8,128)(2,1)S(1)}, u32[]{:S(2)}, u32[]{:S(2)}) collective-permute-start(bf16[520,128]{1,0:T(8,128)(2,1)S(1)} %get-tuple-element.48), channel_id=1, source_target_pairs={{0,8},{8,0},{16,24},{24,16},{1,9},{9,1},{17,25},{25,17},{2,10},{10... | collective-permute-start | bytes 399368 | tf_op jit(solution)/shard_map/ppermute | solution.py:319
  23.8 7.1 %collective-permute-start.8 = (bf16[520,128]{1,0:T(8,128)(2,1)S(1)}, bf16[520,128]{1,0:T(8,128)(2,1)S(1)}, u32[]{:S(2)}, u32[]{:S(2)}) collective-permute-start(bf16[520,128]{1,0:T(8,128)(2,1)S(1)} %get-tuple-element.49), channel_id=1, source_target_pairs={{0,16},{8,24},{16,0},{24,8},{1,17},{9,25},{17,1},{25,9},{2,18},{10... | collective-permute-start | bytes 399368 | tf_op jit(solution)/shard_map/ppermute | solution.py:319
  25.1 9.0 %collective-permute-start.4 = (bf16[256,128]{1,0:T(8,128)(2,1)S(1)}, bf16[256,128]{1,0:T(8,128)(2,1)S(1)}, u32[]{:S(2)}, u32[]{:S(2)}) collective-permute-start(bf16[256,128]{1,0:T(8,128)(2,1)S(1)} %get-tuple-element.45), channel_id=1, source_target_pairs={{0,2},{2,0},{4,6},{6,4},{1,3},{3,1},{5,7},{7,5},{8,10},{10,8},{12,... | collective-permute-start | bytes 196616 | tf_op jit(solution)/shard_map/ppermute | solution.py:319
  25.1 9.2 %collective-permute-start.5 = (bf16[256,128]{1,0:T(8,128)(2,1)S(1)}, bf16[256,128]{1,0:T(8,128)(2,1)S(1)}, u32[]{:S(2)}, u32[]{:S(2)}) collective-permute-start(bf16[256,128]{1,0:T(8,128)(2,1)S(1)} %get-tuple-element.46), channel_id=1, source_target_pairs={{0,4},{2,6},{4,0},{6,2},{1,5},{3,7},{5,1},{7,3},{8,12},{10,14},{12... | collective-permute-start | bytes 196616 | tf_op jit(solution)/shard_map/ppermute | solution.py:319
  26.9 7.4 %collective-permute-start.6 = (bf16[256,128]{1,0:T(8,128)(2,1)S(1)}, bf16[256,128]{1,0:T(8,128)(2,1)S(1)}, u32[]{:S(2)}, u32[]{:S(2)}) collective-permute-start(bf16[256,128]{1,0:T(8,128)(2,1)S(1)} %get-tuple-element.47), channel_id=1, source_target_pairs={{0,6},{2,4},{4,2},{6,0},{1,7},{3,5},{5,3},{7,1},{8,14},{10,12},{12... | collective-permute-start | bytes 196616 | tf_op jit(solution)/shard_map/ppermute | solution.py:319
  31.0 7.6 %collective-permute-start.12 = (bf16[520,128]{1,0:T(8,128)(2,1)S(1)}, bf16[520,128]{1,0:T(8,128)(2,1)S(1)}, u32[]{:S(2)}, u32[]{:S(2)}) collective-permute-start(bf16[520,128]{1,0:T(8,128)(2,1)S(1)} %shard_map.120.refs_4_), channel_id=1, source_target_pairs={{0,96},{32,64},{64,32},{96,0},{1,97},{33,65},{65,33},{97,1},{2,98}... | collective-permute-start | bytes 399368 | tf_op jit(solution)/shard_map/ppermute | solution.py:319
  33.5 5.4 %collective-permute-start.11 = (bf16[520,128]{1,0:T(8,128)(2,1)S(1)}, bf16[520,128]{1,0:T(8,128)(2,1)S(1)}, u32[]{:S(2)}, u32[]{:S(2)}) collective-permute-start(bf16[520,128]{1,0:T(8,128)(2,1)S(1)} %shard_map.120.refs_4_), channel_id=1, source_target_pairs={{0,64},{32,96},{64,0},{96,32},{1,65},{33,97},{65,1},{97,33},{2,66}... | collective-permute-start | bytes 399368 | tf_op jit(solution)/shard_map/ppermute | solution.py:319
  34.0 5.0 %collective-permute-start.10 = (bf16[520,128]{1,0:T(8,128)(2,1)S(1)}, bf16[520,128]{1,0:T(8,128)(2,1)S(1)}, u32[]{:S(2)}, u32[]{:S(2)}) collective-permute-start(bf16[520,128]{1,0:T(8,128)(2,1)S(1)} %shard_map.120.refs_4_), channel_id=1, source_target_pairs={{0,32},{32,0},{64,96},{96,64},{1,33},{33,1},{65,97},{97,65},{2,34}... | collective-permute-start | bytes 399368 | tf_op jit(solution)/shard_map/ppermute | solution.py:319
  38.6 9.2 %copy-start.4 = (f32[128]{0:T(128)S(1)}, f32[128]{0:T(128)}, u32[]{:S(2)}) copy-start(f32[128]{0:T(128)} %param.15) | copy-start | bytes 1540
  39.0 23.8 %slice-start.2 = ((s8[8388608]{0:T(1024)(128)(4,1)}), s8[4194304]{0:T(1024)(128)(4,1)S(1)}, s32[]{:S(2)}) async-start(s8[8388608]{0:T(1024)(128)(4,1)} %bitcast.5), calls=%async_computation.2 | async-start | bytes 8388608
  39.5 3.9 %collective-permute-start.13 = (bf16[520,128]{1,0:T(8,128)(2,1)S(1)}, bf16[520,128]{1,0:T(8,128)(2,1)S(1)}, u32[]{:S(2)}, u32[]{:S(2)}) collective-permute-start(bf16[520,128]{1,0:T(8,128)(2,1)S(1)} %get-tuple-element.51), channel_id=1, source_target_pairs={{0,8},{8,0},{16,24},{24,16},{1,9},{9,1},{17,25},{25,17},{2,10},{10... | collective-permute-start | bytes 399368 | tf_op jit(solution)/shard_map/ppermute | solution.py:319
  39.6 6.8 %collective-permute-start.14 = (bf16[520,128]{1,0:T(8,128)(2,1)S(1)}, bf16[520,128]{1,0:T(8,128)(2,1)S(1)}, u32[]{:S(2)}, u32[]{:S(2)}) collective-permute-start(bf16[520,128]{1,0:T(8,128)(2,1)S(1)} %get-tuple-element.52), channel_id=1, source_target_pairs={{0,16},{8,24},{16,0},{24,8},{1,17},{9,25},{17,1},{25,9},{2,18},{10... | collective-permute-start | bytes 399368 | tf_op jit(solution)/shard_map/ppermute | solution.py:319
  42.5 5.2 %collective-permute-start.15 = (bf16[520,128]{1,0:T(8,128)(2,1)S(1)}, bf16[520,128]{1,0:T(8,128)(2,1)S(1)}, u32[]{:S(2)}, u32[]{:S(2)}) collective-permute-start(bf16[520,128]{1,0:T(8,128)(2,1)S(1)} %get-tuple-element.53), channel_id=1, source_target_pairs={{0,24},{8,16},{16,8},{24,0},{1,25},{9,17},{17,9},{25,1},{2,26},{10... | collective-permute-start | bytes 399368 | tf_op jit(solution)/shard_map/ppermute | solution.py:319
  47.7 15.1 %slice-start = ((s8[8388608]{0:T(1024)(128)(4,1)}), s8[4194304]{0:T(1024)(128)(4,1)S(1)}, s32[]{:S(2)}) async-start(s8[8388608]{0:T(1024)(128)(4,1)} %bitcast.3), calls=%async_computation | async-start | bytes 8388608
  47.8 15.1 %slice-start.3 = ((s8[8388608]{0:T(1024)(128)(4,1)}), s8[4194304]{0:T(1024)(128)(4,1)S(1)}, s32[]{:S(2)}) async-start(s8[8388608]{0:T(1024)(128)(4,1)} %bitcast.5), calls=%async_computation.3 | async-start | bytes 8388608
  49.5 10.0 %collective-permute-start.16 = (bf16[256,128]{1,0:T(8,128)(2,1)S(1)}, bf16[256,128]{1,0:T(8,128)(2,1)S(1)}, u32[]{:S(2)}, u32[]{:S(2)}) collective-permute-start(bf16[256,128]{1,0:T(8,128)(2,1)S(1)} %get-tuple-element.55), channel_id=1, source_target_pairs={{0,3},{1,2},{2,1},{3,0},{4,7},{5,6},{6,5},{7,4},{8,11},{9,10},{10,... | collective-permute-start | bytes 196616 | tf_op jit(solution)/shard_map/ppermute | solution.py:319
  53.0 6.5 %collective-permute-start.17 = (bf16[256,128]{1,0:T(8,128)(2,1)S(1)}, bf16[256,128]{1,0:T(8,128)(2,1)S(1)}, u32[]{:S(2)}, u32[]{:S(2)}) collective-permute-start(bf16[256,128]{1,0:T(8,128)(2,1)S(1)} %get-tuple-element.56), channel_id=1, source_target_pairs={{0,5},{1,4},{2,7},{3,6},{4,1},{5,0},{6,3},{7,2},{8,13},{9,12},{10,... | collective-permute-start | bytes 196616 | tf_op jit(solution)/shard_map/ppermute | solution.py:319
  53.7 7.7 %collective-permute-start.18 = (bf16[256,128]{1,0:T(8,128)(2,1)S(1)}, bf16[256,128]{1,0:T(8,128)(2,1)S(1)}, u32[]{:S(2)}, u32[]{:S(2)}) collective-permute-start(bf16[256,128]{1,0:T(8,128)(2,1)S(1)} %get-tuple-element.57), channel_id=1, source_target_pairs={{0,7},{1,6},{2,5},{3,4},{4,3},{5,2},{6,1},{7,0},{8,15},{9,14},{10,... | collective-permute-start | bytes 196616 | tf_op jit(solution)/shard_map/ppermute | solution.py:319
  61.4 1.5 %collective-permute-start.19 = (bf16[128,512]{1,0:T(8,128)(2,1)S(1)}, bf16[128,512]{1,0:T(8,128)(2,1)S(1)}, u32[]{:S(2)}, u32[]{:S(2)}) collective-permute-start(bf16[128,512]{1,0:T(8,128)(2,1)S(1)} %shard_map.125), channel_id=1, source_target_pairs={{0,1},{1,0},{2,3},{3,2},{4,5},{5,4},{6,7},{7,6},{8,9},{9,8},{10,11... | collective-permute-start | bytes 393224 | tf_op jit(solution)/shard_map/ppermute | solution.py:422
  (5 other events, 21.5 us)

commit v3 on v2

--- a/solution.py
+++ b/solution.py
@@ -139,12 +139,12 @@
             ext[h, HS : 2 * HS, at] = part
             mine = (lane >= HS) if h else (lane < HS)
             vz[h * LEN + k * PAIR : h * LEN + (k + 1) * PAIR, :] = jnp.where(mine, value, zero)
-    for i, (out, k) in enumerate(zip(outs, (1, 2))):
+    for i, (out, k) in enumerate(zip(outs, (2, 3))):
         out[...] = key_piece(ext, vz, phi.at[i], turned.at[i], k)
 
 
 def third_kernel(ext, vz, out, phi, turned):
-    out[...] = key_piece(ext, vz, phi, turned, 3)
+    out[...] = key_piece(ext, vz, phi, turned, 1)
 
 
 def rest_kernel(ext, vz, after, out, phi, turned):
@@ -374,7 +374,7 @@
     own = call(
         rest_kernel, arr(PIECE, 128), spare, [VM] * 2 + [ANY], 8, flops=cost, moved=MIB
     )(ext, vz, third)
-    pieces = exchange([own, first, second, third], "z", ALONG)
+    pieces = exchange([own, third, first, second], "z", ALONG)
     queries = lax.optimization_barrier((queries, third))[0]
     queries = exchange(queries, "y", ALONG)
     inside = call(

time: 67 us -> 67.8 us (1.012)
  waiting for transfers between devices: 16.3 us -> 17.1 us
    ppermute x18, waiting for transfers between devices: 15.3 us -> 16.1 us  [exchange(): moved.append(lax.ppermute(parts[k], axes, pairs[k]))]
where the time goes in v3:
time: 67.8 us; the launch traced here: 67.6 us
  starting transfers between devices  30.9 us (46%)
  Pallas kernels  18.7 us (28%)
  waiting for transfers between devices  17.1 us (25%)
  between operations  0.84 us (1%)
    ppermute x18, starting transfers between devices, exchange(): moved.append(lax.ppermute(parts[k], axes, pairs[k]))  29 us
    ppermute x18, waiting for transfers between devices, exchange(): moved.append(lax.ppermute(parts[k], axes, pairs[k]))  16.1 us
    pallas_call x1, Pallas kernels, body(): call(mlp_kernel, [arr(ROWS, D)] * 2, [], [VM] * 10, 8, flops=2 * 128 * 10...  3.96 us
    pallas_call x1, Pallas kernels, body(): call(features_kernel, arr(NF, 2 * LEN), [pltpu.VMEM((2, 2 * HS, LEN), F32...  2.16 us
    pallas_call x1, Pallas kernels, body(): call(inside_kernel, arr(LEN, 128, dtype=F32), [pltpu.VMEM((LEN, 128), BF)...  2.08 us
    pallas_call x1, Pallas kernels, body(): call(q_kernel, [arr(PAIR, 128)] * 4 + [arr(PAIR, 256)], [pltpu.VMEM((D, 2...  1.91 us
    pallas_call x1, Pallas kernels, body(): call(apply_kernel, [arr(PAIR, 128)] * 3 + [arr(128, NF)], [pltpu.VMEM((NF...  1.72 us
    pallas_call x1, Pallas kernels, body(): call(state_kernel, [arr(PIECE, 128)] * 2 + [arr(2, 2 * HS, LEN, dtype=F32...  1.69 us
  transfers between devices with their start and end apart: 20, of which 10 were waited for; matrix products, arithmetic and copies ran while one was open for 0% of the time, Pallas kernels for 14%

profile of v3, /device:TPU:1, one launch (start us, length us, event | category | flops | bytes accessed | tf_op | source)
XLA Modules:
  0.0 67.6 jit_solution(10910885861455910071)
XLA Ops:
  0.6 1.5 %collective-permute-start = (bf16[128,1024]{1,0:T(8,128)(2,1)}, bf16[128,1024]{1,0:T(8,128)(2,1)S(1)}, u32[]{:S(2)}, u32[]{:S(2)}) collective-permute-start(bf16[128,1024]{1,0:T(8,128)(2,1)} %refs_5_.1), channel_id=1, source_target_pairs={{0,1},{1,0},{2,3},{3,2},{4,5},{5,4},{6,7},{7,6},{8,9},{9,8},{10,11... | collective-permute-start | bytes 786440 | tf_op jit(solution)/shard_map/ppermute | solution.py:328
  2.1 1.6 %shard_map.113 = (bf16[128,1024]{1,0:T(8,128)(2,1)S(1)}, f32[1,1024]{1,0:T(1,128)S(1)}, bf16[3,1024,256]{2,1,0:T(8,128)(2,1)S(1)}) custom-call(bf16[128,1024]{1,0:T(8,128)(2,1)} %refs_5_.1, f32[1,1024]{1,0:T(1,128)} %bitcast.10, bf16[1024,1024]{1,0:T(8,128)(2,1)} %wk.3, bf16[1024,1024]{1,0:T(8,128)(2,1)} %wv.3), custom_call_target="tpu_custom_call" | custom-call | flops 134217728 | bytes 4194304 | tf_op jit(solution)/shard_map/pallas_call | solution.py:329
  4.4 1.5 %collective-permute-start.1 = (bf16[256,256]{1,0:T(8,128)(2,1)S(1)}, bf16[256,256]{1,0:T(8,128)(2,1)S(1)}, u32[]{:S(2)}, u32[]{:S(2)}) collective-permute-start(bf16[256,256]{1,0:T(8,128)(2,1)S(1)} %get-tuple-element.39), channel_id=1, source_target_pairs={{0,2},{2,0},{4,6},{6,4},{1,3},{3,1},{5,7},{7,5},{8,10},{10,8},{12,... | collective-permute-start | bytes 393224 | tf_op jit(solution)/shard_map/ppermute | solution.py:319
  5.9 2.6 %collective-permute-start.2 = (bf16[256,256]{1,0:T(8,128)(2,1)S(1)}, bf16[256,256]{1,0:T(8,128)(2,1)S(1)}, u32[]{:S(2)}, u32[]{:S(2)}) collective-permute-start(bf16[256,256]{1,0:T(8,128)(2,1)S(1)} %get-tuple-element.40), channel_id=1, source_target_pairs={{0,4},{2,6},{4,0},{6,2},{1,5},{3,7},{5,1},{7,3},{8,12},{10,14},{12... | collective-permute-start | bytes 393224 | tf_op jit(solution)/shard_map/ppermute | solution.py:319
  8.6 1.9 %shard_map.115 = (bf16[256,128]{1,0:T(8,128)(2,1)S(1)}, bf16[256,128]{1,0:T(8,128)(2,1)S(1)}, bf16[256,128]{1,0:T(8,128)(2,1)S(1)}, bf16[256,128]{1,0:T(8,128)(2,1)S(1)}, bf16[256,256]{1,0:T(8,128)(2,1)S(1)}) custom-call(bf16[256,1024]{1,0:T(8,128)(2,1)S(1)} %get-tuple-element.33.normed, bf16[1024,1024]{1,0:T(8,128)(2,1)S(1)} %copy-done, ...), custom_call_target="tpu_custom_call" | custom-call | flops 268435456 | bytes 4194304 | tf_op jit(solution)/shard_map/pallas_call | solution.py:352
  10.5 4.4 %collective-permute-done.2.refs_2_ = bf16[256,256]{1,0:T(8,128)(2,1)S(1)} collective-permute-done((bf16[256,256]{1,0:T(8,128)(2,1)S(1)}, bf16[256,256]{1,0:T(8,128)(2,1)S(1)}, u32[]{:S(2)}, u32[]{:S(2)}) %collective-permute-start.2) | collective-permute-done | bytes 131104 | tf_op jit(solution)/shard_map/ppermute | solution.py:319
  14.9 2.5 %collective-permute-done.3.refs_3_ = bf16[256,256]{1,0:T(8,128)(2,1)S(1)} collective-permute-done((bf16[256,256]{1,0:T(8,128)(2,1)S(1)}, bf16[256,256]{1,0:T(8,128)(2,1)S(1)}, u32[]{:S(2)}, u32[]{:S(2)}) %collective-permute-start.3) | collective-permute-done | bytes 131104 | tf_op jit(solution)/shard_map/ppermute | solution.py:319
  17.5 1.7 %shard_map.116 = (bf16[520,128]{1,0:T(8,128)(2,1)S(1)}, bf16[520,128]{1,0:T(8,128)(2,1)S(1)}, f32[2,128,1024]{2,1,0:T(8,128)S(1)}, bf16[2048,128]{1,0:T(8,128)(2,1)S(1)}) custom-call(bf16[256,256]{1,0:T(8,128)(2,1)S(1)} %get-tuple-element.38.refs_0_, bf16[256,256]{1,0:T(8,128)(2,1)S(1)} %collective-permute-done.1.refs_1_, ...), custom_call_target="tpu_custom_call" | custom-call | flops 1090519040 | bytes 2097152 | tf_op jit(solution)/shard_map/pallas_call | solution.py:364
  20.0 1.7 %collective-permute-start.7 = (bf16[520,128]{1,0:T(8,128)(2,1)S(1)}, bf16[520,128]{1,0:T(8,128)(2,1)S(1)}, u32[]{:S(2)}, u32[]{:S(2)}) collective-permute-start(bf16[520,128]{1,0:T(8,128)(2,1)S(1)} %shard_map.117.after), channel_id=1, source_target_pairs={{0,8},{8,0},{16,24},{24,16},{1,9},{9,1},{17,25},{25,17},{2,10},{10... | collective-permute-start | bytes 399368 | tf_op jit(solution)/shard_map/ppermute | solution.py:319
  21.7 3.3 %collective-permute-start.8 = (bf16[520,128]{1,0:T(8,128)(2,1)S(1)}, bf16[520,128]{1,0:T(8,128)(2,1)S(1)}, u32[]{:S(2)}, u32[]{:S(2)}) collective-permute-start(bf16[520,128]{1,0:T(8,128)(2,1)S(1)} %get-tuple-element.48), channel_id=1, source_target_pairs={{0,16},{8,24},{16,0},{24,8},{1,17},{9,25},{17,1},{25,9},{2,18},{10... | collective-permute-start | bytes 399368 | tf_op jit(solution)/shard_map/ppermute | solution.py:319
  26.2 2.6 %collective-permute-start.6 = (bf16[256,128]{1,0:T(8,128)(2,1)S(1)}, bf16[256,128]{1,0:T(8,128)(2,1)S(1)}, u32[]{:S(2)}, u32[]{:S(2)}) collective-permute-start(bf16[256,128]{1,0:T(8,128)(2,1)S(1)} %get-tuple-element.47), channel_id=1, source_target_pairs={{0,6},{2,4},{4,2},{6,0},{1,7},{3,5},{5,3},{7,1},{8,14},{10,12},{12... | collective-permute-start | bytes 196616 | tf_op jit(solution)/shard_map/ppermute | solution.py:319
  30.6 2.6 %collective-permute-done.9.refs_3_ = bf16[520,128]{1,0:T(8,128)(2,1)S(1)} collective-permute-done((bf16[520,128]{1,0:T(8,128)(2,1)S(1)}, bf16[520,128]{1,0:T(8,128)(2,1)S(1)}, u32[]{:S(2)}, u32[]{:S(2)}) %collective-permute-start.9) | collective-permute-done | bytes 133152 | tf_op jit(solution)/shard_map/ppermute | solution.py:319
  33.3 2.5 %collective-permute-start.12 = (bf16[520,128]{1,0:T(8,128)(2,1)S(1)}, bf16[520,128]{1,0:T(8,128)(2,1)S(1)}, u32[]{:S(2)}, u32[]{:S(2)}) collective-permute-start(bf16[520,128]{1,0:T(8,128)(2,1)S(1)} %shard_map.120.refs_4_), channel_id=1, source_target_pairs={{0,96},{32,64},{64,32},{96,0},{1,97},{33,65},{65,33},{97,1},{2,98}... | collective-permute-start | bytes 399368 | tf_op jit(solution)/shard_map/ppermute | solution.py:319
  36.6 2.2 %shard_map.118.refs_8_.refs_0_.phi = bf16[2080,2048]{1,0:T(8,128)(2,1)S(1)} custom-call(bf16[256,128]{1,0:T(8,128)(2,1)S(1)} %get-tuple-element.44.refs_0_.refs_4_, bf16[256,128]{1,0:T(8,128)(2,1)S(1)} %collective-permute-done.4.refs_1_.refs_5_, bf16[256,128]{1,0:T(8,128)(2,1)S(1)} %collective-permute-done.5.refs_2_.refs_6_, ...), custom_call_target="tpu_custom_call" | custom-call | flops 545259520 | bytes 9437184 | tf_op jit(solution)/shard_map/pallas_call | solution.py:392
  38.8 2.1 %shard_map.121.refs_9_.refs_5_.inside = f32[1024,128]{1,0:T(8,128)S(1)} custom-call(bf16[256,256]{1,0:T(8,128)(2,1)S(1)} %get-tuple-element.38.refs_0_, bf16[256,256]{1,0:T(8,128)(2,1)S(1)} %collective-permute-done.1.refs_1_, bf16[256,256]{1,0:T(8,128)(2,1)S(1)} %collective-permute-done.2.refs_2_, bf16[256,256]{1,0:T(8,128)(2,1)S(1)} %collective-permute-done.3.refs_3_, ...), custom_call_target="tpu_custom_call" | custom-call | flops 1073741824 | bytes 2097152 | tf_op jit(solution)/shard_map/pallas_call | solution.py:380
  42.2 1.7 %collective-permute-start.14 = (bf16[520,128]{1,0:T(8,128)(2,1)S(1)}, bf16[520,128]{1,0:T(8,128)(2,1)S(1)}, u32[]{:S(2)}, u32[]{:S(2)}) collective-permute-start(bf16[520,128]{1,0:T(8,128)(2,1)S(1)} %get-tuple-element.52), channel_id=1, source_target_pairs={{0,16},{8,24},{16,0},{24,8},{1,17},{9,25},{17,1},{25,9},{2,18},{10... | collective-permute-start | bytes 399368 | tf_op jit(solution)/shard_map/ppermute | solution.py:319
  44.0 2.1 %collective-permute-start.15 = (bf16[520,128]{1,0:T(8,128)(2,1)S(1)}, bf16[520,128]{1,0:T(8,128)(2,1)S(1)}, u32[]{:S(2)}, u32[]{:S(2)}) collective-permute-start(bf16[520,128]{1,0:T(8,128)(2,1)S(1)} %get-tuple-element.53), channel_id=1, source_target_pairs={{0,24},{8,16},{16,8},{24,0},{1,25},{9,17},{17,9},{25,1},{2,26},{10... | collective-permute-start | bytes 399368 | tf_op jit(solution)/shard_map/ppermute | solution.py:319
  46.1 1.7 %collective-permute-done.14.refs_3_ = bf16[520,128]{1,0:T(8,128)(2,1)S(1)} collective-permute-done((bf16[520,128]{1,0:T(8,128)(2,1)S(1)}, bf16[520,128]{1,0:T(8,128)(2,1)S(1)}, u32[]{:S(2)}, u32[]{:S(2)}) %collective-permute-start.14) | collective-permute-done | bytes 133152 | tf_op jit(solution)/shard_map/ppermute | solution.py:319
  47.8 1.4 %collective-permute-done.15.refs_4_ = bf16[520,128]{1,0:T(8,128)(2,1)S(1)} collective-permute-done((bf16[520,128]{1,0:T(8,128)(2,1)S(1)}, bf16[520,128]{1,0:T(8,128)(2,1)S(1)}, u32[]{:S(2)}, u32[]{:S(2)}) %collective-permute-start.15) | collective-permute-done | bytes 133152 | tf_op jit(solution)/shard_map/ppermute | solution.py:319
  49.2 1.7 %shard_map.123 = (bf16[256,128]{1,0:T(8,128)(2,1)S(1)}, bf16[256,128]{1,0:T(8,128)(2,1)S(1)}, bf16[256,128]{1,0:T(8,128)(2,1)S(1)}, bf16[128,2080]{1,0:T(8,128)(2,1)S(1)}) custom-call(bf16[2080,2048]{1,0:T(8,128)(2,1)S(1)} %shard_map.118.refs_8_.refs_0_.phi, bf16[520,128]{1,0:T(8,128)(2,1)S(1)} %get-tuple-element.50.refs_1_, ...), custom_call_target="tpu_custom_call" | custom-call | flops 1635778560 | bytes 2097152 | tf_op jit(solution)/shard_map/pallas_call | solution.py:407
  50.9 2.8 %collective-permute-start.16 = (bf16[256,128]{1,0:T(8,128)(2,1)S(1)}, bf16[256,128]{1,0:T(8,128)(2,1)S(1)}, u32[]{:S(2)}, u32[]{:S(2)}) collective-permute-start(bf16[256,128]{1,0:T(8,128)(2,1)S(1)} %get-tuple-element.55), channel_id=1, source_target_pairs={{0,3},{1,2},{2,1},{3,0},{4,7},{5,6},{6,5},{7,4},{8,11},{9,10},{10,... | collective-permute-start | bytes 196616 | tf_op jit(solution)/shard_map/ppermute | solution.py:319
  54.3 5.3 %collective-permute-start.18 = (bf16[256,128]{1,0:T(8,128)(2,1)S(1)}, bf16[256,128]{1,0:T(8,128)(2,1)S(1)}, u32[]{:S(2)}, u32[]{:S(2)}) collective-permute-start(bf16[256,128]{1,0:T(8,128)(2,1)S(1)} %get-tuple-element.57), channel_id=1, source_target_pairs={{0,7},{1,6},{2,5},{3,4},{4,3},{5,2},{6,1},{7,0},{8,15},{9,14},{10,... | collective-permute-start | bytes 196616 | tf_op jit(solution)/shard_map/ppermute | solution.py:319
  60.4 1.7 %collective-permute-done.18.refs_3_ = bf16[256,128]{1,0:T(8,128)(2,1)S(1)} collective-permute-done((bf16[256,128]{1,0:T(8,128)(2,1)S(1)}, bf16[256,128]{1,0:T(8,128)(2,1)S(1)}, u32[]{:S(2)}, u32[]{:S(2)}) %collective-permute-start.18) | collective-permute-done | bytes 65568 | tf_op jit(solution)/shard_map/ppermute | solution.py:319
  63.7 4.0 %shard_map.126 = (bf16[128,1024]{1,0:T(8,128)(2,1)}, bf16[128,1024]{1,0:T(8,128)(2,1)}) custom-call(bf16[256,128]{1,0:T(8,128)(2,1)S(1)} %shard_map.124.refs_0_, bf16[256,128]{1,0:T(8,128)(2,1)S(1)} %collective-permute-done.16.refs_1_, bf16[256,128]{1,0:T(8,128)(2,1)S(1)} %collective-permute-done.17.refs_2_, ...), custom_call_target="tpu_custom_call" | custom-call | flops 2415919104 | bytes 18874368 | tf_op jit(solution)/shard_map/pallas_call | solution.py:424
  (50 shorter events, 9.5 us)
Async XLA Ops:
  0.6 3.1 %collective-permute-start = (bf16[128,1024]{1,0:T(8,128)(2,1)}, bf16[128,1024]{1,0:T(8,128)(2,1)S(1)}, u32[]{:S(2)}, u32[]{:S(2)}) collective-permute-start(bf16[128,1024]{1,0:T(8,128)(2,1)} %refs_5_.1), channel_id=1, source_target_pairs={{0,1},{1,0},{2,3},{3,2},{4,5},{5,4},{6,7},{7,6},{8,9},{9,8},{10,11... | collective-permute-start | bytes 786440 | tf_op jit(solution)/shard_map/ppermute | solution.py:328
  4.4 6.0 %collective-permute-start.1 = (bf16[256,256]{1,0:T(8,128)(2,1)S(1)}, bf16[256,256]{1,0:T(8,128)(2,1)S(1)}, u32[]{:S(2)}, u32[]{:S(2)}) collective-permute-start(bf16[256,256]{1,0:T(8,128)(2,1)S(1)} %get-tuple-element.39), channel_id=1, source_target_pairs={{0,2},{2,0},{4,6},{6,4},{1,3},{3,1},{5,7},{7,5},{8,10},{10,8},{12,... | collective-permute-start | bytes 393224 | tf_op jit(solution)/shard_map/ppermute | solution.py:319
  5.9 9.0 %collective-permute-start.2 = (bf16[256,256]{1,0:T(8,128)(2,1)S(1)}, bf16[256,256]{1,0:T(8,128)(2,1)S(1)}, u32[]{:S(2)}, u32[]{:S(2)}) collective-permute-start(bf16[256,256]{1,0:T(8,128)(2,1)S(1)} %get-tuple-element.40), channel_id=1, source_target_pairs={{0,4},{2,6},{4,0},{6,2},{1,5},{3,7},{5,1},{7,3},{8,12},{10,14},{12... | collective-permute-start | bytes 393224 | tf_op jit(solution)/shard_map/ppermute | solution.py:319
  8.6 8.9 %collective-permute-start.3 = (bf16[256,256]{1,0:T(8,128)(2,1)S(1)}, bf16[256,256]{1,0:T(8,128)(2,1)S(1)}, u32[]{:S(2)}, u32[]{:S(2)}) collective-permute-start(bf16[256,256]{1,0:T(8,128)(2,1)S(1)} %get-tuple-element.41), channel_id=1, source_target_pairs={{0,6},{2,4},{4,2},{6,0},{1,7},{3,5},{5,3},{7,1},{8,14},{10,12},{12... | collective-permute-start | bytes 393224 | tf_op jit(solution)/shard_map/ppermute | solution.py:319
  20.0 6.3 %collective-permute-start.7 = (bf16[520,128]{1,0:T(8,128)(2,1)S(1)}, bf16[520,128]{1,0:T(8,128)(2,1)S(1)}, u32[]{:S(2)}, u32[]{:S(2)}) collective-permute-start(bf16[520,128]{1,0:T(8,128)(2,1)S(1)} %shard_map.117.after), channel_id=1, source_target_pairs={{0,8},{8,0},{16,24},{24,16},{1,9},{9,1},{17,25},{25,17},{2,10},{10... | collective-permute-start | bytes 399368 | tf_op jit(solution)/shard_map/ppermute | solution.py:319
  21.7 9.0 %collective-permute-start.8 = (bf16[520,128]{1,0:T(8,128)(2,1)S(1)}, bf16[520,128]{1,0:T(8,128)(2,1)S(1)}, u32[]{:S(2)}, u32[]{:S(2)}) collective-permute-start(bf16[520,128]{1,0:T(8,128)(2,1)S(1)} %get-tuple-element.48), channel_id=1, source_target_pairs={{0,16},{8,24},{16,0},{24,8},{1,17},{9,25},{17,1},{25,9},{2,18},{10... | collective-permute-start | bytes 399368 | tf_op jit(solution)/shard_map/ppermute | solution.py:319
  25.0 8.2 %collective-permute-start.9 = (bf16[520,128]{1,0:T(8,128)(2,1)S(1)}, bf16[520,128]{1,0:T(8,128)(2,1)S(1)}, u32[]{:S(2)}, u32[]{:S(2)}) collective-permute-start(bf16[520,128]{1,0:T(8,128)(2,1)S(1)} %get-tuple-element.49), channel_id=1, source_target_pairs={{0,24},{8,16},{16,8},{24,0},{1,25},{9,17},{17,9},{25,1},{2,26},{10... | collective-permute-start | bytes 399368 | tf_op jit(solution)/shard_map/ppermute | solution.py:319
  25.0 11.4 %collective-permute-start.4 = (bf16[256,128]{1,0:T(8,128)(2,1)S(1)}, bf16[256,128]{1,0:T(8,128)(2,1)S(1)}, u32[]{:S(2)}, u32[]{:S(2)}) collective-permute-start(bf16[256,128]{1,0:T(8,128)(2,1)S(1)} %get-tuple-element.45), channel_id=1, source_target_pairs={{0,2},{2,0},{4,6},{6,4},{1,3},{3,1},{5,7},{7,5},{8,10},{10,8},{12,... | collective-permute-start | bytes 196616 | tf_op jit(solution)/shard_map/ppermute | solution.py:319
  25.0 11.6 %collective-permute-start.5 = (bf16[256,128]{1,0:T(8,128)(2,1)S(1)}, bf16[256,128]{1,0:T(8,128)(2,1)S(1)}, u32[]{:S(2)}, u32[]{:S(2)}) collective-permute-start(bf16[256,128]{1,0:T(8,128)(2,1)S(1)} %get-tuple-element.46), channel_id=1, source_target_pairs={{0,4},{2,6},{4,0},{6,2},{1,5},{3,7},{5,1},{7,3},{8,12},{10,14},{12... | collective-permute-start | bytes 196616 | tf_op jit(solution)/shard_map/ppermute | solution.py:319
  26.2 10.4 %collective-permute-start.6 = (bf16[256,128]{1,0:T(8,128)(2,1)S(1)}, bf16[256,128]{1,0:T(8,128)(2,1)S(1)}, u32[]{:S(2)}, u32[]{:S(2)}) collective-permute-start(bf16[256,128]{1,0:T(8,128)(2,1)S(1)} %get-tuple-element.47), channel_id=1, source_target_pairs={{0,6},{2,4},{4,2},{6,0},{1,7},{3,5},{5,3},{7,1},{8,14},{10,12},{12... | collective-permute-start | bytes 196616 | tf_op jit(solution)/shard_map/ppermute | solution.py:319
  33.3 7.6 %collective-permute-start.12 = (bf16[520,128]{1,0:T(8,128)(2,1)S(1)}, bf16[520,128]{1,0:T(8,128)(2,1)S(1)}, u32[]{:S(2)}, u32[]{:S(2)}) collective-permute-start(bf16[520,128]{1,0:T(8,128)(2,1)S(1)} %shard_map.120.refs_4_), channel_id=1, source_target_pairs={{0,96},{32,64},{64,32},{96,0},{1,97},{33,65},{65,33},{97,1},{2,98}... | collective-permute-start | bytes 399368 | tf_op jit(solution)/shard_map/ppermute | solution.py:319
  35.8 5.4 %collective-permute-start.11 = (bf16[520,128]{1,0:T(8,128)(2,1)S(1)}, bf16[520,128]{1,0:T(8,128)(2,1)S(1)}, u32[]{:S(2)}, u32[]{:S(2)}) collective-permute-start(bf16[520,128]{1,0:T(8,128)(2,1)S(1)} %shard_map.120.refs_4_), channel_id=1, source_target_pairs={{0,64},{32,96},{64,0},{96,32},{1,65},{33,97},{65,1},{97,33},{2,66}... | collective-permute-start | bytes 399368 | tf_op jit(solution)/shard_map/ppermute | solution.py:319
  36.4 5.3 %collective-permute-start.10 = (bf16[520,128]{1,0:T(8,128)(2,1)S(1)}, bf16[520,128]{1,0:T(8,128)(2,1)S(1)}, u32[]{:S(2)}, u32[]{:S(2)}) collective-permute-start(bf16[520,128]{1,0:T(8,128)(2,1)S(1)} %shard_map.120.refs_4_), channel_id=1, source_target_pairs={{0,32},{32,0},{64,96},{96,64},{1,33},{33,1},{65,97},{97,65},{2,34}... | collective-permute-start | bytes 399368 | tf_op jit(solution)/shard_map/ppermute | solution.py:319
  40.9 8.3 %copy-start.4 = (f32[128]{0:T(128)S(1)}, f32[128]{0:T(128)}, u32[]{:S(2)}) copy-start(f32[128]{0:T(128)} %param.15) | copy-start | bytes 1540
  41.7 21.9 %slice-start.2 = ((s8[8388608]{0:T(1024)(128)(4,1)}), s8[4194304]{0:T(1024)(128)(4,1)S(1)}, s32[]{:S(2)}) async-start(s8[8388608]{0:T(1024)(128)(4,1)} %bitcast.5), calls=%async_computation.2 | async-start | bytes 8388608
  42.1 3.9 %collective-permute-start.13 = (bf16[520,128]{1,0:T(8,128)(2,1)S(1)}, bf16[520,128]{1,0:T(8,128)(2,1)S(1)}, u32[]{:S(2)}, u32[]{:S(2)}) collective-permute-start(bf16[520,128]{1,0:T(8,128)(2,1)S(1)} %get-tuple-element.51), channel_id=1, source_target_pairs={{0,8},{8,0},{16,24},{24,16},{1,9},{9,1},{17,25},{25,17},{2,10},{10... | collective-permute-start | bytes 399368 | tf_op jit(solution)/shard_map/ppermute | solution.py:319
  42.2 5.6 %collective-permute-start.14 = (bf16[520,128]{1,0:T(8,128)(2,1)S(1)}, bf16[520,128]{1,0:T(8,128)(2,1)S(1)}, u32[]{:S(2)}, u32[]{:S(2)}) collective-permute-start(bf16[520,128]{1,0:T(8,128)(2,1)S(1)} %get-tuple-element.52), channel_id=1, source_target_pairs={{0,16},{8,24},{16,0},{24,8},{1,17},{9,25},{17,1},{25,9},{2,18},{10... | collective-permute-start | bytes 399368 | tf_op jit(solution)/shard_map/ppermute | solution.py:319
  44.0 5.2 %collective-permute-start.15 = (bf16[520,128]{1,0:T(8,128)(2,1)S(1)}, bf16[520,128]{1,0:T(8,128)(2,1)S(1)}, u32[]{:S(2)}, u32[]{:S(2)}) collective-permute-start(bf16[520,128]{1,0:T(8,128)(2,1)S(1)} %get-tuple-element.53), channel_id=1, source_target_pairs={{0,24},{8,16},{16,8},{24,0},{1,25},{9,17},{17,9},{25,1},{2,26},{10... | collective-permute-start | bytes 399368 | tf_op jit(solution)/shard_map/ppermute | solution.py:319
  49.2 14.4 %slice-start = ((s8[8388608]{0:T(1024)(128)(4,1)}), s8[4194304]{0:T(1024)(128)(4,1)S(1)}, s32[]{:S(2)}) async-start(s8[8388608]{0:T(1024)(128)(4,1)} %bitcast.3), calls=%async_computation | async-start | bytes 8388608
  49.2 14.4 %slice-start.3 = ((s8[8388608]{0:T(1024)(128)(4,1)}), s8[4194304]{0:T(1024)(128)(4,1)S(1)}, s32[]{:S(2)}) async-start(s8[8388608]{0:T(1024)(128)(4,1)} %bitcast.5), calls=%async_computation.3 | async-start | bytes 8388608
  50.9 9.5 %collective-permute-start.16 = (bf16[256,128]{1,0:T(8,128)(2,1)S(1)}, bf16[256,128]{1,0:T(8,128)(2,1)S(1)}, u32[]{:S(2)}, u32[]{:S(2)}) collective-permute-start(bf16[256,128]{1,0:T(8,128)(2,1)S(1)} %get-tuple-element.55), channel_id=1, source_target_pairs={{0,3},{1,2},{2,1},{3,0},{4,7},{5,6},{6,5},{7,4},{8,11},{9,10},{10,... | collective-permute-start | bytes 196616 | tf_op jit(solution)/shard_map/ppermute | solution.py:319
  53.7 6.7 %collective-permute-start.17 = (bf16[256,128]{1,0:T(8,128)(2,1)S(1)}, bf16[256,128]{1,0:T(8,128)(2,1)S(1)}, u32[]{:S(2)}, u32[]{:S(2)}) collective-permute-start(bf16[256,128]{1,0:T(8,128)(2,1)S(1)} %get-tuple-element.56), channel_id=1, source_target_pairs={{0,5},{1,4},{2,7},{3,6},{4,1},{5,0},{6,3},{7,2},{8,13},{9,12},{10,... | collective-permute-start | bytes 196616 | tf_op jit(solution)/shard_map/ppermute | solution.py:319
  54.3 7.8 %collective-permute-start.18 = (bf16[256,128]{1,0:T(8,128)(2,1)S(1)}, bf16[256,128]{1,0:T(8,128)(2,1)S(1)}, u32[]{:S(2)}, u32[]{:S(2)}) collective-permute-start(bf16[256,128]{1,0:T(8,128)(2,1)S(1)} %get-tuple-element.57), channel_id=1, source_target_pairs={{0,7},{1,6},{2,5},{3,4},{4,3},{5,2},{6,1},{7,0},{8,15},{9,14},{10,... | collective-permute-start | bytes 196616 | tf_op jit(solution)/shard_map/ppermute | solution.py:319
  62.1 1.5 %collective-permute-start.19 = (bf16[128,512]{1,0:T(8,128)(2,1)S(1)}, bf16[128,512]{1,0:T(8,128)(2,1)S(1)}, u32[]{:S(2)}, u32[]{:S(2)}) collective-permute-start(bf16[128,512]{1,0:T(8,128)(2,1)S(1)} %shard_map.125), channel_id=1, source_target_pairs={{0,1},{1,0},{2,3},{3,2},{4,5},{5,4},{6,7},{7,6},{8,9},{9,8},{10,11... | collective-permute-start | bytes 393224 | tf_op jit(solution)/shard_map/ppermute | solution.py:422
  (5 other events, 20.7 us)

commit v4 on v2

--- a/solution.py
+++ b/solution.py
@@ -193,7 +193,7 @@
 
 
 def combine_kernel(*refs):
-    pieces, totals, outs = refs[:4], refs[4:8], refs[10:14]
+    pieces, totals, outs = refs[:4], refs[4:8], refs[9:13]
     x, z = lax.axis_index("x"), lax.axis_index("z")
     base = jnp.zeros((PIECE, 128), F32)
     for k in range(1, 4):
@@ -399,8 +399,8 @@
         moved=9 * MIB,
     )(*queries)
     states = call(
-        combine_kernel, [arr(PIECE, 128)] * 4, [], [VM] * 8 + [ANY] * 2, 8, moved=MIB
-    )(*pieces, *totals, phi, inside)
+        combine_kernel, [arr(PIECE, 128)] * 4, [], [VM] * 8 + [ANY], 8, moved=MIB
+    )(*pieces, *totals, phi)
     states = exchange(states, "z", ALONG)
 
     scale = head_gain.reshape(1, 128)

time: 67 us -> 70.4 us (1.051)
  waiting for transfers between devices: 16.3 us -> 22.3 us
  starting transfers between devices: 30.9 us -> 28.3 us
    ppermute x18, waiting for transfers between devices: 15.3 us -> 21.3 us  [exchange(): moved.append(lax.ppermute(parts[k], axes, pairs[k]))]
    ppermute x18, starting transfers between devices: 29 us -> 26.4 us  [exchange(): moved.append(lax.ppermute(parts[k], axes, pairs[k]))]
  transfers between devices with their start and end apart: 20 -> 20, of which waited for: 10 -> 12; matrix products, arithmetic and copies ran while one was open for 0% -> 0% of each run, Pallas kernels for 14% -> 13%
where the time goes in v4:
time: 70.4 us; the launch traced here: 70.2 us
  starting transfers between devices  28.3 us (40%)
  waiting for transfers between devices  22.3 us (32%)
  Pallas kernels  18.7 us (27%)
  between operations  0.85 us (1%)
    ppermute x18, starting transfers between devices, exchange(): moved.append(lax.ppermute(parts[k], axes, pairs[k]))  26.4 us
    ppermute x18, waiting for transfers between devices, exchange(): moved.append(lax.ppermute(parts[k], axes, pairs[k]))  21.3 us
    pallas_call x1, Pallas kernels, body(): call(mlp_kernel, [arr(ROWS, D)] * 2, [], [VM] * 10, 8, flops=2 * 128 * 10...  3.97 us
    pallas_call x1, Pallas kernels, body(): call(features_kernel, arr(NF, 2 * LEN), [pltpu.VMEM((2, 2 * HS, LEN), F32...  2.16 us
    pallas_call x1, Pallas kernels, body(): call(inside_kernel, arr(LEN, 128, dtype=F32), [pltpu.VMEM((LEN, 128), BF)...  2.08 us
    pallas_call x1, Pallas kernels, body(): call(q_kernel, [arr(PAIR, 128)] * 4 + [arr(PAIR, 256)], [pltpu.VMEM((D, 2...  1.91 us
    pallas_call x1, Pallas kernels, body(): call(apply_kernel, [arr(PAIR, 128)] * 3 + [arr(128, NF)], [pltpu.VMEM((NF...  1.71 us
    pallas_call x1, Pallas kernels, body(): call(state_kernel, [arr(PIECE, 128)] * 2 + [arr(2, 2 * HS, LEN, dtype=F32...  1.71 us
  transfers between devices with their start and end apart: 20, of which 12 were waited for; matrix products, arithmetic and copies ran while one was open for 0% of the time, Pallas kernels for 13%

profile of v4, /device:TPU:1, one launch (start us, length us, event | category | flops | bytes accessed | tf_op | source)
XLA Modules:
  0.0 70.2 jit_solution(1732632624254397411)
XLA Ops:
  0.6 1.5 %collective-permute-start = (bf16[128,1024]{1,0:T(8,128)(2,1)}, bf16[128,1024]{1,0:T(8,128)(2,1)S(1)}, u32[]{:S(2)}, u32[]{:S(2)}) collective-permute-start(bf16[128,1024]{1,0:T(8,128)(2,1)} %refs_5_.1), channel_id=1, source_target_pairs={{0,1},{1,0},{2,3},{3,2},{4,5},{5,4},{6,7},{7,6},{8,9},{9,8},{10,11... | collective-permute-start | bytes 786440 | tf_op jit(solution)/shard_map/ppermute | solution.py:328
  2.1 1.6 %shard_map.113 = (bf16[128,1024]{1,0:T(8,128)(2,1)S(1)}, f32[1,1024]{1,0:T(1,128)S(1)}, bf16[3,1024,256]{2,1,0:T(8,128)(2,1)S(1)}) custom-call(bf16[128,1024]{1,0:T(8,128)(2,1)} %refs_5_.1, f32[1,1024]{1,0:T(1,128)} %bitcast.10, bf16[1024,1024]{1,0:T(8,128)(2,1)} %wk.3, bf16[1024,1024]{1,0:T(8,128)(2,1)} %wv.3), custom_call_target="tpu_custom_call" | custom-call | flops 134217728 | bytes 4194304 | tf_op jit(solution)/shard_map/pallas_call | solution.py:329
  4.4 1.5 %collective-permute-start.1 = (bf16[256,256]{1,0:T(8,128)(2,1)S(1)}, bf16[256,256]{1,0:T(8,128)(2,1)S(1)}, u32[]{:S(2)}, u32[]{:S(2)}) collective-permute-start(bf16[256,256]{1,0:T(8,128)(2,1)S(1)} %get-tuple-element.39), channel_id=1, source_target_pairs={{0,2},{2,0},{4,6},{6,4},{1,3},{3,1},{5,7},{7,5},{8,10},{10,8},{12,... | collective-permute-start | bytes 393224 | tf_op jit(solution)/shard_map/ppermute | solution.py:319
  5.9 2.6 %collective-permute-start.2 = (bf16[256,256]{1,0:T(8,128)(2,1)S(1)}, bf16[256,256]{1,0:T(8,128)(2,1)S(1)}, u32[]{:S(2)}, u32[]{:S(2)}) collective-permute-start(bf16[256,256]{1,0:T(8,128)(2,1)S(1)} %get-tuple-element.40), channel_id=1, source_target_pairs={{0,4},{2,6},{4,0},{6,2},{1,5},{3,7},{5,1},{7,3},{8,12},{10,14},{12... | collective-permute-start | bytes 393224 | tf_op jit(solution)/shard_map/ppermute | solution.py:319
  8.6 1.9 %shard_map.115 = (bf16[256,128]{1,0:T(8,128)(2,1)S(1)}, bf16[256,128]{1,0:T(8,128)(2,1)S(1)}, bf16[256,128]{1,0:T(8,128)(2,1)S(1)}, bf16[256,128]{1,0:T(8,128)(2,1)S(1)}, bf16[256,256]{1,0:T(8,128)(2,1)S(1)}) custom-call(bf16[256,1024]{1,0:T(8,128)(2,1)S(1)} %get-tuple-element.33.normed, bf16[1024,1024]{1,0:T(8,128)(2,1)S(1)} %copy-done, ...), custom_call_target="tpu_custom_call" | custom-call | flops 268435456 | bytes 4194304 | tf_op jit(solution)/shard_map/pallas_call | solution.py:352
  10.5 4.4 %collective-permute-done.2.refs_2_ = bf16[256,256]{1,0:T(8,128)(2,1)S(1)} collective-permute-done((bf16[256,256]{1,0:T(8,128)(2,1)S(1)}, bf16[256,256]{1,0:T(8,128)(2,1)S(1)}, u32[]{:S(2)}, u32[]{:S(2)}) %collective-permute-start.2) | collective-permute-done | bytes 131104 | tf_op jit(solution)/shard_map/ppermute | solution.py:319
  14.9 2.5 %collective-permute-done.3.refs_3_ = bf16[256,256]{1,0:T(8,128)(2,1)S(1)} collective-permute-done((bf16[256,256]{1,0:T(8,128)(2,1)S(1)}, bf16[256,256]{1,0:T(8,128)(2,1)S(1)}, u32[]{:S(2)}, u32[]{:S(2)}) %collective-permute-start.3) | collective-permute-done | bytes 131104 | tf_op jit(solution)/shard_map/ppermute | solution.py:319
  17.5 1.7 %shard_map.116 = (bf16[520,128]{1,0:T(8,128)(2,1)S(1)}, bf16[520,128]{1,0:T(8,128)(2,1)S(1)}, f32[2,128,1024]{2,1,0:T(8,128)S(1)}, bf16[2048,128]{1,0:T(8,128)(2,1)S(1)}) custom-call(bf16[256,256]{1,0:T(8,128)(2,1)S(1)} %get-tuple-element.38.refs_0_, bf16[256,256]{1,0:T(8,128)(2,1)S(1)} %collective-permute-done.1.refs_1_, ...), custom_call_target="tpu_custom_call" | custom-call | flops 1090519040 | bytes 2097152 | tf_op jit(solution)/shard_map/pallas_call | solution.py:364
  20.0 3.8 %collective-permute-start.9 = (bf16[520,128]{1,0:T(8,128)(2,1)S(1)}, bf16[520,128]{1,0:T(8,128)(2,1)S(1)}, u32[]{:S(2)}, u32[]{:S(2)}) collective-permute-start(bf16[520,128]{1,0:T(8,128)(2,1)S(1)} %shard_map.117.after), channel_id=1, source_target_pairs={{0,24},{8,16},{16,8},{24,0},{1,25},{9,17},{17,9},{25,1},{2,26},{10... | collective-permute-start | bytes 399368 | tf_op jit(solution)/shard_map/ppermute | solution.py:319
  23.8 1.3 %collective-permute-start.8 = (bf16[520,128]{1,0:T(8,128)(2,1)S(1)}, bf16[520,128]{1,0:T(8,128)(2,1)S(1)}, u32[]{:S(2)}, u32[]{:S(2)}) collective-permute-start(bf16[520,128]{1,0:T(8,128)(2,1)S(1)} %get-tuple-element.49), channel_id=1, source_target_pairs={{0,16},{8,24},{16,0},{24,8},{1,17},{9,25},{17,1},{25,9},{2,18},{10... | collective-permute-start | bytes 399368 | tf_op jit(solution)/shard_map/ppermute | solution.py:319
  26.9 1.0 %collective-permute-done.7.refs_1_ = bf16[520,128]{1,0:T(8,128)(2,1)S(1)} collective-permute-done((bf16[520,128]{1,0:T(8,128)(2,1)S(1)}, bf16[520,128]{1,0:T(8,128)(2,1)S(1)}, u32[]{:S(2)}, u32[]{:S(2)}) %collective-permute-start.7) | collective-permute-done | bytes 133152 | tf_op jit(solution)/shard_map/ppermute | solution.py:319
  27.9 3.0 %collective-permute-done.8.refs_2_ = bf16[520,128]{1,0:T(8,128)(2,1)S(1)} collective-permute-done((bf16[520,128]{1,0:T(8,128)(2,1)S(1)}, bf16[520,128]{1,0:T(8,128)(2,1)S(1)}, u32[]{:S(2)}, u32[]{:S(2)}) %collective-permute-start.8) | collective-permute-done | bytes 133152 | tf_op jit(solution)/shard_map/ppermute | solution.py:319
  31.0 2.5 %collective-permute-start.12 = (bf16[520,128]{1,0:T(8,128)(2,1)S(1)}, bf16[520,128]{1,0:T(8,128)(2,1)S(1)}, u32[]{:S(2)}, u32[]{:S(2)}) collective-permute-start(bf16[520,128]{1,0:T(8,128)(2,1)S(1)} %shard_map.120.refs_4_), channel_id=1, source_target_pairs={{0,96},{32,64},{64,32},{96,0},{1,97},{33,65},{65,33},{97,1},{2,98}... | collective-permute-start | bytes 399368 | tf_op jit(solution)/shard_map/ppermute | solution.py:319
  34.6 4.4 %collective-permute-done.5.refs_2_.refs_6_ = bf16[256,128]{1,0:T(8,128)(2,1)S(1)} collective-permute-done((bf16[256,128]{1,0:T(8,128)(2,1)S(1)}, bf16[256,128]{1,0:T(8,128)(2,1)S(1)}, u32[]{:S(2)}, u32[]{:S(2)}) %collective-permute-start.5) | collective-permute-done | bytes 65568 | tf_op jit(solution)/shard_map/ppermute | solution.py:319
  39.6 2.2 %shard_map.118.refs_8_.refs_0_.phi = bf16[2080,2048]{1,0:T(8,128)(2,1)S(1)} custom-call(bf16[256,128]{1,0:T(8,128)(2,1)S(1)} %get-tuple-element.44.refs_0_.refs_4_, bf16[256,128]{1,0:T(8,128)(2,1)S(1)} %collective-permute-done.4.refs_1_.refs_5_, bf16[256,128]{1,0:T(8,128)(2,1)S(1)} %collective-permute-done.5.refs_2_.refs_6_, ...), custom_call_target="tpu_custom_call" | custom-call | flops 545259520 | bytes 9437184 | tf_op jit(solution)/shard_map/pallas_call | solution.py:392
  42.4 3.0 %collective-permute-start.14 = (bf16[520,128]{1,0:T(8,128)(2,1)S(1)}, bf16[520,128]{1,0:T(8,128)(2,1)S(1)}, u32[]{:S(2)}, u32[]{:S(2)}) collective-permute-start(bf16[520,128]{1,0:T(8,128)(2,1)S(1)} %get-tuple-element.52), channel_id=1, source_target_pairs={{0,16},{8,24},{16,0},{24,8},{1,17},{9,25},{17,1},{25,9},{2,18},{10... | collective-permute-start | bytes 399368 | tf_op jit(solution)/shard_map/ppermute | solution.py:319
  46.2 2.1 %shard_map.122.refs_5_.inside = f32[1024,128]{1,0:T(8,128)S(1)} custom-call(bf16[256,256]{1,0:T(8,128)(2,1)S(1)} %get-tuple-element.38.refs_0_, bf16[256,256]{1,0:T(8,128)(2,1)S(1)} %collective-permute-done.1.refs_1_, bf16[256,256]{1,0:T(8,128)(2,1)S(1)} %collective-permute-done.2.refs_2_, bf16[256,256]{1,0:T(8,128)(2,1)S(1)} %collective-permute-done.3.refs_3_, ...), custom_call_target="tpu_custom_call" | custom-call | flops 1073741824 | bytes 2097152 | tf_op jit(solution)/shard_map/pallas_call | solution.py:380
  49.2 1.4 %collective-permute-done.15.refs_4_ = bf16[520,128]{1,0:T(8,128)(2,1)S(1)} collective-permute-done((bf16[520,128]{1,0:T(8,128)(2,1)S(1)}, bf16[520,128]{1,0:T(8,128)(2,1)S(1)}, u32[]{:S(2)}, u32[]{:S(2)}) %collective-permute-start.15) | collective-permute-done | bytes 133152 | tf_op jit(solution)/shard_map/ppermute | solution.py:319
  50.6 1.7 %shard_map.123 = (bf16[256,128]{1,0:T(8,128)(2,1)S(1)}, bf16[256,128]{1,0:T(8,128)(2,1)S(1)}, bf16[256,128]{1,0:T(8,128)(2,1)S(1)}, bf16[128,2080]{1,0:T(8,128)(2,1)S(1)}) custom-call(bf16[2080,2048]{1,0:T(8,128)(2,1)S(1)} %shard_map.118.refs_8_.refs_0_.phi, bf16[520,128]{1,0:T(8,128)(2,1)S(1)} %get-tuple-element.50.refs_1_, ...), custom_call_target="tpu_custom_call" | custom-call | flops 1635778560 | bytes 2097152 | tf_op jit(solution)/shard_map/pallas_call | solution.py:407
  52.4 4.7 %collective-permute-start.16 = (bf16[256,128]{1,0:T(8,128)(2,1)S(1)}, bf16[256,128]{1,0:T(8,128)(2,1)S(1)}, u32[]{:S(2)}, u32[]{:S(2)}) collective-permute-start(bf16[256,128]{1,0:T(8,128)(2,1)S(1)} %get-tuple-element.55), channel_id=1, source_target_pairs={{0,3},{1,2},{2,1},{3,0},{4,7},{5,6},{6,5},{7,4},{8,11},{9,10},{10,... | collective-permute-start | bytes 196616 | tf_op jit(solution)/shard_map/ppermute | solution.py:319
  57.1 2.2 %collective-permute-start.17 = (bf16[256,128]{1,0:T(8,128)(2,1)S(1)}, bf16[256,128]{1,0:T(8,128)(2,1)S(1)}, u32[]{:S(2)}, u32[]{:S(2)}) collective-permute-start(bf16[256,128]{1,0:T(8,128)(2,1)S(1)} %get-tuple-element.56), channel_id=1, source_target_pairs={{0,5},{1,4},{2,7},{3,6},{4,1},{5,0},{6,3},{7,2},{8,13},{9,12},{10,... | collective-permute-start | bytes 196616 | tf_op jit(solution)/shard_map/ppermute | solution.py:319
  59.2 2.7 %collective-permute-start.18 = (bf16[256,128]{1,0:T(8,128)(2,1)S(1)}, bf16[256,128]{1,0:T(8,128)(2,1)S(1)}, u32[]{:S(2)}, u32[]{:S(2)}) collective-permute-start(bf16[256,128]{1,0:T(8,128)(2,1)S(1)} %get-tuple-element.57), channel_id=1, source_target_pairs={{0,7},{1,6},{2,5},{3,4},{4,3},{5,2},{6,1},{7,0},{8,15},{9,14},{10,... | collective-permute-start | bytes 196616 | tf_op jit(solution)/shard_map/ppermute | solution.py:319
  63.2 1.5 %collective-permute-done.18.refs_3_ = bf16[256,128]{1,0:T(8,128)(2,1)S(1)} collective-permute-done((bf16[256,128]{1,0:T(8,128)(2,1)S(1)}, bf16[256,128]{1,0:T(8,128)(2,1)S(1)}, u32[]{:S(2)}, u32[]{:S(2)}) %collective-permute-start.18) | collective-permute-done | bytes 65568 | tf_op jit(solution)/shard_map/ppermute | solution.py:319
  66.3 4.0 %shard_map.126 = (bf16[128,1024]{1,0:T(8,128)(2,1)}, bf16[128,1024]{1,0:T(8,128)(2,1)}) custom-call(bf16[256,128]{1,0:T(8,128)(2,1)S(1)} %shard_map.124.refs_0_, bf16[256,128]{1,0:T(8,128)(2,1)S(1)} %collective-permute-done.16.refs_1_, bf16[256,128]{1,0:T(8,128)(2,1)S(1)} %collective-permute-done.17.refs_2_, ...), custom_call_target="tpu_custom_call" | custom-call | flops 2415919104 | bytes 18874368 | tf_op jit(solution)/shard_map/pallas_call | solution.py:424
  (50 shorter events, 10.1 us)
Async XLA Ops:
  0.6 3.1 %collective-permute-start = (bf16[128,1024]{1,0:T(8,128)(2,1)}, bf16[128,1024]{1,0:T(8,128)(2,1)S(1)}, u32[]{:S(2)}, u32[]{:S(2)}) collective-permute-start(bf16[128,1024]{1,0:T(8,128)(2,1)} %refs_5_.1), channel_id=1, source_target_pairs={{0,1},{1,0},{2,3},{3,2},{4,5},{5,4},{6,7},{7,6},{8,9},{9,8},{10,11... | collective-permute-start | bytes 786440 | tf_op jit(solution)/shard_map/ppermute | solution.py:328
  4.4 6.0 %collective-permute-start.1 = (bf16[256,256]{1,0:T(8,128)(2,1)S(1)}, bf16[256,256]{1,0:T(8,128)(2,1)S(1)}, u32[]{:S(2)}, u32[]{:S(2)}) collective-permute-start(bf16[256,256]{1,0:T(8,128)(2,1)S(1)} %get-tuple-element.39), channel_id=1, source_target_pairs={{0,2},{2,0},{4,6},{6,4},{1,3},{3,1},{5,7},{7,5},{8,10},{10,8},{12,... | collective-permute-start | bytes 393224 | tf_op jit(solution)/shard_map/ppermute | solution.py:319
  5.9 9.0 %collective-permute-start.2 = (bf16[256,256]{1,0:T(8,128)(2,1)S(1)}, bf16[256,256]{1,0:T(8,128)(2,1)S(1)}, u32[]{:S(2)}, u32[]{:S(2)}) collective-permute-start(bf16[256,256]{1,0:T(8,128)(2,1)S(1)} %get-tuple-element.40), channel_id=1, source_target_pairs={{0,4},{2,6},{4,0},{6,2},{1,5},{3,7},{5,1},{7,3},{8,12},{10,14},{12... | collective-permute-start | bytes 393224 | tf_op jit(solution)/shard_map/ppermute | solution.py:319
  8.6 8.9 %collective-permute-start.3 = (bf16[256,256]{1,0:T(8,128)(2,1)S(1)}, bf16[256,256]{1,0:T(8,128)(2,1)S(1)}, u32[]{:S(2)}, u32[]{:S(2)}) collective-permute-start(bf16[256,256]{1,0:T(8,128)(2,1)S(1)} %get-tuple-element.41), channel_id=1, source_target_pairs={{0,6},{2,4},{4,2},{6,0},{1,7},{3,5},{5,3},{7,1},{8,14},{10,12},{12... | collective-permute-start | bytes 393224 | tf_op jit(solution)/shard_map/ppermute | solution.py:319
  20.0 6.9 %collective-permute-start.9 = (bf16[520,128]{1,0:T(8,128)(2,1)S(1)}, bf16[520,128]{1,0:T(8,128)(2,1)S(1)}, u32[]{:S(2)}, u32[]{:S(2)}) collective-permute-start(bf16[520,128]{1,0:T(8,128)(2,1)S(1)} %shard_map.117.after), channel_id=1, source_target_pairs={{0,24},{8,16},{16,8},{24,0},{1,25},{9,17},{17,9},{25,1},{2,26},{10... | collective-permute-start | bytes 399368 | tf_op jit(solution)/shard_map/ppermute | solution.py:319
  23.8 4.1 %collective-permute-start.7 = (bf16[520,128]{1,0:T(8,128)(2,1)S(1)}, bf16[520,128]{1,0:T(8,128)(2,1)S(1)}, u32[]{:S(2)}, u32[]{:S(2)}) collective-permute-start(bf16[520,128]{1,0:T(8,128)(2,1)S(1)} %get-tuple-element.48), channel_id=1, source_target_pairs={{0,8},{8,0},{16,24},{24,16},{1,9},{9,1},{17,25},{25,17},{2,10},{10... | collective-permute-start | bytes 399368 | tf_op jit(solution)/shard_map/ppermute | solution.py:319
  23.8 7.1 %collective-permute-start.8 = (bf16[520,128]{1,0:T(8,128)(2,1)S(1)}, bf16[520,128]{1,0:T(8,128)(2,1)S(1)}, u32[]{:S(2)}, u32[]{:S(2)}) collective-permute-start(bf16[520,128]{1,0:T(8,128)(2,1)S(1)} %get-tuple-element.49), channel_id=1, source_target_pairs={{0,16},{8,24},{16,0},{24,8},{1,17},{9,25},{17,1},{25,9},{2,18},{10... | collective-permute-start | bytes 399368 | tf_op jit(solution)/shard_map/ppermute | solution.py:319
  25.1 9.2 %collective-permute-start.4 = (bf16[256,128]{1,0:T(8,128)(2,1)S(1)}, bf16[256,128]{1,0:T(8,128)(2,1)S(1)}, u32[]{:S(2)}, u32[]{:S(2)}) collective-permute-start(bf16[256,128]{1,0:T(8,128)(2,1)S(1)} %get-tuple-element.45), channel_id=1, source_target_pairs={{0,2},{2,0},{4,6},{6,4},{1,3},{3,1},{5,7},{7,5},{8,10},{10,8},{12,... | collective-permute-start | bytes 196616 | tf_op jit(solution)/shard_map/ppermute | solution.py:319
  31.0 10.8 %collective-permute-start.12 = (bf16[520,128]{1,0:T(8,128)(2,1)S(1)}, bf16[520,128]{1,0:T(8,128)(2,1)S(1)}, u32[]{:S(2)}, u32[]{:S(2)}) collective-permute-start(bf16[520,128]{1,0:T(8,128)(2,1)S(1)} %shard_map.120.refs_4_), channel_id=1, source_target_pairs={{0,96},{32,64},{64,32},{96,0},{1,97},{33,65},{65,33},{97,1},{2,98}... | collective-permute-start | bytes 399368 | tf_op jit(solution)/shard_map/ppermute | solution.py:319
  33.5 8.3 %collective-permute-start.11 = (bf16[520,128]{1,0:T(8,128)(2,1)S(1)}, bf16[520,128]{1,0:T(8,128)(2,1)S(1)}, u32[]{:S(2)}, u32[]{:S(2)}) collective-permute-start(bf16[520,128]{1,0:T(8,128)(2,1)S(1)} %shard_map.120.refs_4_), channel_id=1, source_target_pairs={{0,64},{32,96},{64,0},{96,32},{1,65},{33,97},{65,1},{97,33},{2,66}... | collective-permute-start | bytes 399368 | tf_op jit(solution)/shard_map/ppermute | solution.py:319
  34.0 7.8 %collective-permute-start.10 = (bf16[520,128]{1,0:T(8,128)(2,1)S(1)}, bf16[520,128]{1,0:T(8,128)(2,1)S(1)}, u32[]{:S(2)}, u32[]{:S(2)}) collective-permute-start(bf16[520,128]{1,0:T(8,128)(2,1)S(1)} %shard_map.120.refs_4_), channel_id=1, source_target_pairs={{0,32},{32,0},{64,96},{96,64},{1,33},{33,1},{65,97},{97,65},{2,34}... | collective-permute-start | bytes 399368 | tf_op jit(solution)/shard_map/ppermute | solution.py:319
  34.3 4.7 %collective-permute-start.5 = (bf16[256,128]{1,0:T(8,128)(2,1)S(1)}, bf16[256,128]{1,0:T(8,128)(2,1)S(1)}, u32[]{:S(2)}, u32[]{:S(2)}) collective-permute-start(bf16[256,128]{1,0:T(8,128)(2,1)S(1)} %get-tuple-element.46), channel_id=1, source_target_pairs={{0,4},{2,6},{4,0},{6,2},{1,5},{3,7},{5,1},{7,3},{8,12},{10,14},{12... | collective-permute-start | bytes 196616 | tf_op jit(solution)/shard_map/ppermute | solution.py:319
  34.3 5.3 %collective-permute-start.6 = (bf16[256,128]{1,0:T(8,128)(2,1)S(1)}, bf16[256,128]{1,0:T(8,128)(2,1)S(1)}, u32[]{:S(2)}, u32[]{:S(2)}) collective-permute-start(bf16[256,128]{1,0:T(8,128)(2,1)S(1)} %get-tuple-element.47), channel_id=1, source_target_pairs={{0,6},{2,4},{4,2},{6,0},{1,7},{3,5},{5,3},{7,1},{8,14},{10,12},{12... | collective-permute-start | bytes 196616 | tf_op jit(solution)/shard_map/ppermute | solution.py:319
  42.3 8.4 %copy-start.4 = (f32[128]{0:T(128)S(1)}, f32[128]{0:T(128)}, u32[]{:S(2)}) copy-start(f32[128]{0:T(128)} %param.15) | copy-start | bytes 1540
  42.3 6.0 %collective-permute-start.13 = (bf16[520,128]{1,0:T(8,128)(2,1)S(1)}, bf16[520,128]{1,0:T(8,128)(2,1)S(1)}, u32[]{:S(2)}, u32[]{:S(2)}) collective-permute-start(bf16[520,128]{1,0:T(8,128)(2,1)S(1)} %get-tuple-element.51), channel_id=1, source_target_pairs={{0,8},{8,0},{16,24},{24,16},{1,9},{9,1},{17,25},{25,17},{2,10},{10... | collective-permute-start | bytes 399368 | tf_op jit(solution)/shard_map/ppermute | solution.py:319
  42.4 6.9 %collective-permute-start.14 = (bf16[520,128]{1,0:T(8,128)(2,1)S(1)}, bf16[520,128]{1,0:T(8,128)(2,1)S(1)}, u32[]{:S(2)}, u32[]{:S(2)}) collective-permute-start(bf16[520,128]{1,0:T(8,128)(2,1)S(1)} %get-tuple-element.52), channel_id=1, source_target_pairs={{0,16},{8,24},{16,0},{24,8},{1,17},{9,25},{17,1},{25,9},{2,18},{10... | collective-permute-start | bytes 399368 | tf_op jit(solution)/shard_map/ppermute | solution.py:319
  45.4 5.2 %collective-permute-start.15 = (bf16[520,128]{1,0:T(8,128)(2,1)S(1)}, bf16[520,128]{1,0:T(8,128)(2,1)S(1)}, u32[]{:S(2)}, u32[]{:S(2)}) collective-permute-start(bf16[520,128]{1,0:T(8,128)(2,1)S(1)} %get-tuple-element.53), channel_id=1, source_target_pairs={{0,24},{8,16},{16,8},{24,0},{1,25},{9,17},{17,9},{25,1},{2,26},{10... | collective-permute-start | bytes 399368 | tf_op jit(solution)/shard_map/ppermute | solution.py:319
  46.2 20.0 %slice-start.2 = ((s8[8388608]{0:T(1024)(128)(4,1)}), s8[4194304]{0:T(1024)(128)(4,1)S(1)}, s32[]{:S(2)}) async-start(s8[8388608]{0:T(1024)(128)(4,1)} %bitcast.5), calls=%async_computation.2 | async-start | bytes 8388608
  50.6 15.6 %slice-start = ((s8[8388608]{0:T(1024)(128)(4,1)}), s8[4194304]{0:T(1024)(128)(4,1)S(1)}, s32[]{:S(2)}) async-start(s8[8388608]{0:T(1024)(128)(4,1)} %bitcast.3), calls=%async_computation | async-start | bytes 8388608
  50.6 15.6 %slice-start.3 = ((s8[8388608]{0:T(1024)(128)(4,1)}), s8[4194304]{0:T(1024)(128)(4,1)S(1)}, s32[]{:S(2)}) async-start(s8[8388608]{0:T(1024)(128)(4,1)} %bitcast.5), calls=%async_computation.3 | async-start | bytes 8388608
  52.4 10.3 %collective-permute-start.16 = (bf16[256,128]{1,0:T(8,128)(2,1)S(1)}, bf16[256,128]{1,0:T(8,128)(2,1)S(1)}, u32[]{:S(2)}, u32[]{:S(2)}) collective-permute-start(bf16[256,128]{1,0:T(8,128)(2,1)S(1)} %get-tuple-element.55), channel_id=1, source_target_pairs={{0,3},{1,2},{2,1},{3,0},{4,7},{5,6},{6,5},{7,4},{8,11},{9,10},{10,... | collective-permute-start | bytes 196616 | tf_op jit(solution)/shard_map/ppermute | solution.py:319
  57.1 6.1 %collective-permute-start.17 = (bf16[256,128]{1,0:T(8,128)(2,1)S(1)}, bf16[256,128]{1,0:T(8,128)(2,1)S(1)}, u32[]{:S(2)}, u32[]{:S(2)}) collective-permute-start(bf16[256,128]{1,0:T(8,128)(2,1)S(1)} %get-tuple-element.56), channel_id=1, source_target_pairs={{0,5},{1,4},{2,7},{3,6},{4,1},{5,0},{6,3},{7,2},{8,13},{9,12},{10,... | collective-permute-start | bytes 196616 | tf_op jit(solution)/shard_map/ppermute | solution.py:319
  59.2 5.5 %collective-permute-start.18 = (bf16[256,128]{1,0:T(8,128)(2,1)S(1)}, bf16[256,128]{1,0:T(8,128)(2,1)S(1)}, u32[]{:S(2)}, u32[]{:S(2)}) collective-permute-start(bf16[256,128]{1,0:T(8,128)(2,1)S(1)} %get-tuple-element.57), channel_id=1, source_target_pairs={{0,7},{1,6},{2,5},{3,4},{4,3},{5,2},{6,1},{7,0},{8,15},{9,14},{10,... | collective-permute-start | bytes 196616 | tf_op jit(solution)/shard_map/ppermute | solution.py:319
  64.8 1.5 %collective-permute-start.19 = (bf16[128,512]{1,0:T(8,128)(2,1)S(1)}, bf16[128,512]{1,0:T(8,128)(2,1)S(1)}, u32[]{:S(2)}, u32[]{:S(2)}) collective-permute-start(bf16[128,512]{1,0:T(8,128)(2,1)S(1)} %shard_map.125), channel_id=1, source_target_pairs={{0,1},{1,0},{2,3},{3,2},{4,5},{5,4},{6,7},{7,6},{8,9},{9,8},{10,11... | collective-permute-start | bytes 393224 | tf_op jit(solution)/shard_map/ppermute | solution.py:422
  (5 other events, 21.9 us)
